TPU v7x, 32 devices: a whole 2x2x4 slice. The times are simulated.
32 devices in a mesh: chain: 2 (over y), cell: 4 (over z), col: 4 (over x, core).
Axes of the slice: x: 2, y: 2, z: 4, core: 2. Of those that a mesh axis runs over, the one named last changes fastest.
Arguments:
- grad: float32 [16384, 64], P(('chain', 'cell', 'col')), parts along dimension 0, may hold values from -6 to 6
- near_tiles: bfloat16 [4, 2, 2048, 2048], P('cell', None, 'col'), may hold values from -0.09375 to 0.09375
- tile_count: int32 [4], replicated, may hold values from 1 to 2
- near_offset: int32 [4], replicated, may hold values from -2 to 2, as said below
- far_src: int32 [4, 8], replicated, may hold values from 0 to 3
- far_count: int32 [4], replicated, may hold values from 1 to 8
- far_cores: float32 [4, 8, 64, 64], P('cell'), may hold values from -0.25 to 0.25
- basis_out: bfloat16 [8192, 64], P(('cell', 'col')), may hold values from -0.75 to 0.75
- basis_in: bfloat16 [8192, 64], P(('cell', 'col')), may hold values from -0.125 to 0.125
Outputs:
- step_block: float32 [16384, 64], P(('chain', 'cell', 'col')), parts along dimension 0
There are 2 independent parts, one for each index of `chain`. A program takes and returns all parts, laid end to end along the dimension named above; an argument that names none is the same for every part. Nothing has to cross between parts.
Inputs may be any that keep to these rules, and one draw needn't show every extreme that they name: c + near_offset[c] is a cluster of the chain, and near_offset[c] is never 0.
All inputs are finite; a program needn't handle non-finite values.
Results may differ from a plain program's by a relative error of at most 0.0035.
Values may be sent and summed in bfloat16 or wider, within the bound.
No kernel may reach another device: no remote copies, remote signals or barrier semaphores. Data moves between devices by JAX's collectives and lax.ppermute only.
A program may use at most 64 MiB of HBM per device.

v0:
```python
import jax
import jax.numpy as jnp
from jax import lax
from jax.sharding import PartitionSpec as P


def shifted(value, axis, by):
    devices = lax.axis_size(axis)
    pairs = [(i, i + by) for i in range(devices) if 0 <= i + by < devices]
    return lax.ppermute(value, axis, pairs)


def pick_offset(stacked, offset):
    position = offset + 2 - (offset > 0).astype(jnp.int32)
    return lax.dynamic_index_in_dim(stacked, position, 0, keepdims=False)


def coupling(table, sources, count, cores):
    picked = jnp.take(table, sources, axis=0)
    slots = jnp.arange(cores.shape[0], dtype=jnp.int32)
    masked = jnp.where((slots < count)[:, None, None], cores, jnp.zeros_like(cores))
    return jnp.einsum("kab,kbw->aw", masked, picked, precision=lax.Precision.HIGHEST)


def body(
    grad, near_tiles, tile_count, near_offset, far_src, far_count, far_cores, basis_out, basis_in
):
    owner = lax.axis_index("cell")
    rounded = grad.astype(jnp.bfloat16)
    offset = near_offset[owner]
    steps_list = (-2, -1, 1, 2)
    whole = lax.all_gather(rounded, "col", axis=0, tiled=True)
    moved = [shifted(whole, "cell", -step) for step in steps_list]
    beside = pick_offset(jnp.stack(moved), offset)
    tiles = near_tiles[0]
    own_term = jnp.dot(tiles[0], whole, preferred_element_type=jnp.float32)
    other_term = jnp.dot(tiles[1], beside, preferred_element_type=jnp.float32)
    near = own_term + jnp.where(tile_count[owner] == 2, other_term, jnp.zeros_like(other_term))
    partial_proj = lax.dot_general(
        basis_in, rounded, (((0,), (0,)), ((), ())), preferred_element_type=jnp.float32
    )
    sources = far_src[owner]
    count = far_count[owner]
    cores = far_cores[0]
    proj = lax.psum(partial_proj, "col")
    table = lax.all_gather(proj[None], "cell", axis=0, tiled=True)
    core_block = coupling(table, sources, count, cores).astype(jnp.bfloat16)
    far = jnp.dot(basis_out, core_block, preferred_element_type=jnp.float32)
    return near + far


def solution(mesh):
    placed = (
        P(("chain", "cell", "col"), None),
        P("cell", None, "col", None),
        P(),
        P(),
        P(),
        P(),
        P("cell", None, None, None),
        P(("cell", "col"), None),
        P(("cell", "col"), None),
    )
    return jax.shard_map(
        body,
        mesh=mesh,
        in_specs=placed,
        out_specs=P(("chain", "cell", "col"), None),
        check_vma=False,
    )
```

profile of v0, /device:TPU:0, one launch (start us, length us, event | category | flops | bytes accessed | tf_op | source)
XLA Modules:
  0.0 60.8 jit_solution(2780922674257491303)
XLA Ops:
  0.0 0.0 copy-start
  0.0 0.9 %convert_element_type.10 = bf16[512,64]{0,1:T(8,128)(2,1)S(1)} convert(f32[512,64]{0,1:T(8,128)} %param.9) | non-fusion elementwise | flops 32768 | bytes 196608 | tf_op jit(solution)/shard_map/convert_element_type | solution.py:29
  1.0 7.2 %all_gather.6 = bf16[2048,64]{0,1:T(8,128)(2,1)S(1)} all-gather(bf16[512,64]{0,1:T(8,128)(2,1)S(1)} %convert_element_type.10), channel_id=1, replica_groups=mesh['chain'=2,'cell'=4,'col'=4] {'col'}, dimensions={0}, use_global_device_ids=true | all-gather | bytes 327680 | tf_op jit(solution)/shard_map/all_gather | solution.py:32
  8.2 4.5 %collective-permute-start = (bf16[2048,64]{0,1:T(8,128)(2,1)S(1)}, bf16[2048,64]{0,1:T(8,128)(2,1)S(1)}, u32[]{:S(2)}, u32[]{:S(2)}) collective-permute-start(bf16[2048,64]{0,1:T(8,128)(2,1)S(1)} %all_gather.6), channel_id=1, source_target_pairs={{0,8},{4,12},{1,9},{5,13},{2,10},{6,14},{3,11},{7,15},{16,24},{20,... | collective-permute-start | bytes 786440 | tf_op jit(solution)/shard_map/ppermute | solution.py:10
  12.7 3.5 %collective-permute-start.1 = (bf16[2048,64]{0,1:T(8,128)(2,1)S(1)}, bf16[2048,64]{0,1:T(8,128)(2,1)S(1)}, u32[]{:S(2)}, u32[]{:S(2)}) collective-permute-start(bf16[2048,64]{0,1:T(8,128)(2,1)S(1)} %all_gather.6), channel_id=1, source_target_pairs={{0,4},{4,8},{8,12},{1,5},{5,9},{9,13},{2,6},{6,10},{10,14},{3,7},{... | collective-permute-start | bytes 786440 | tf_op jit(solution)/shard_map/ppermute | solution.py:10
  16.2 1.3 %collective-permute-start.2 = (bf16[2048,64]{0,1:T(8,128)(2,1)S(1)}, bf16[2048,64]{0,1:T(8,128)(2,1)S(1)}, u32[]{:S(2)}, u32[]{:S(2)}) collective-permute-start(bf16[2048,64]{0,1:T(8,128)(2,1)S(1)} %all_gather.6), channel_id=1, source_target_pairs={{4,0},{8,4},{12,8},{5,1},{9,5},{13,9},{6,2},{10,6},{14,10},{7,3},{... | collective-permute-start | bytes 786440 | tf_op jit(solution)/shard_map/ppermute | solution.py:10
  17.5 1.3 %collective-permute-start.3 = (bf16[2048,64]{0,1:T(8,128)(2,1)S(1)}, bf16[2048,64]{0,1:T(8,128)(2,1)S(1)}, u32[]{:S(2)}, u32[]{:S(2)}) collective-permute-start(bf16[2048,64]{0,1:T(8,128)(2,1)S(1)} %all_gather.6), channel_id=1, source_target_pairs={{8,0},{12,4},{9,1},{13,5},{10,2},{14,6},{11,3},{15,7},{24,16},{28,... | collective-permute-start | bytes 786440 | tf_op jit(solution)/shard_map/ppermute | solution.py:10
  18.8 1.2 %dynamic_slice.19 = s32[1]{0:T(128)} dynamic-slice(s32[4]{0:T(128)} %param.14, s32[]{:T(128)S(6)} %select_n.45), dynamic_slice_sizes={1} | dynamic-slice | bytes 12 | tf_op jit(solution)/shard_map/dynamic_slice | solution.py:43
  20.1 0.7 %fusion.30 = s32[8]{0:T(128)S(1)} fusion(s32[4,8]{1,0:T(4,128)} %param.13, s32[]{:T(128)S(6)} %select_n.45), kind=kLoop, calls=%fused_computation.35 | loop fusion | flops 24 | bytes 68 | tf_op jit(solution)/shard_map/jit(_take)/jit(_where)/select_n | solution.py:19
  20.8 1.3 %compare_and_fusion = (pred[8]{0:T(512)(128)(4,1)S(1)}, pred[8]{0:T(512)(128)(4,1)S(1)}) fusion(s32[4,8]{1,0:T(4,128)} %param.13, s32[]{:T(128)S(6)} %select_n.45, s32[]{:T(128)} %bitcast.10), kind=kLoop, calls=%fused_computation.32 | loop fusion | flops 56 | bytes 56 | tf_op jit(solution)/shard_map/jit(_take)/and | solution.py:19
  22.1 1.0 %convolution_bitcast_fusion.1 = f32[1,64,64]{2,1,0:T(8,128)S(1)} fusion(bf16[512,64]{0,1:T(8,128)(2,1)} %param.17, bf16[512,64]{0,1:T(8,128)(2,1)S(1)} %convert_element_type.10), kind=kOutput, calls=%fused_computation.12 | convolution fusion | flops 4194304 | bytes 147456 | tf_op jit(solution)/shard_map/dot_general | solution.py:39
  23.1 11.4 %psum.7 = f32[1,64,64]{2,1,0:T(8,128)S(1)} all-reduce(f32[1,64,64]{2,1,0:T(8,128)S(1)} %convolution_bitcast_fusion.1), channel_id=1, replica_groups=mesh['chain'=2,'cell'=4,'col'=4] {'col'}, use_global_device_ids=true, to_apply=%region_0.1 | all-reduce | flops 4096 | bytes 32768 | tf_op jit(solution)/shard_map/psum | solution.py:45
  34.5 14.3 %all_gather.7 = f32[4,64,64]{2,1,0:T(8,128)S(1)} all-gather(f32[1,64,64]{2,1,0:T(8,128)S(1)} %psum.7), channel_id=1, replica_groups=mesh['chain'=2,'cell'=4,'col'=4] {'cell'}, dimensions={0}, use_global_device_ids=true | all-gather | bytes 81920 | tf_op jit(solution)/shard_map/all_gather | solution.py:46
  48.8 0.6 gather_fusion
  49.3 1.4 %fusion.18 = bf16[64,64]{1,0:T(8,128)(2,1)S(1)} fusion(f32[1,8,64,64]{3,2,1,0:T(8,128)} %param.15, f32[8,64,64]{2,1,0:T(8,128)S(1)} %gather_fusion, pred[8]{0:T(512)(128)(4,1)S(1)} %get-tuple-element.5, pred[8]{0:T(512)(128)(4,1)S(1)} %get-tuple-element.6), kind=kOutput, calls=%fused_computation.14 | convolution fusion | flops 25235456 | bytes 270352 | tf_op jit(solution)/shard_map/kab,kbw->aw/dot_general | solution.py:22
  50.8 1.2 %dynamic_slice.17 = s32[1]{0:T(128)} dynamic-slice(s32[4]{0:T(128)} %param.12, s32[]{:T(128)S(6)} %select_n.45), dynamic_slice_sizes={1} | dynamic-slice | bytes 12 | tf_op jit(solution)/shard_map/dynamic_slice | solution.py:30
  53.3 1.3 %dynamic_slice.16 = s32[1]{0:T(128)} dynamic-slice(s32[4]{0:T(128)} %param.11, s32[]{:T(128)S(6)} %select_n.45), dynamic_slice_sizes={1} | dynamic-slice | bytes 12 | tf_op jit(solution)/shard_map/dynamic_slice | solution.py:38
  55.2 0.2 convolution_bitcast_fusion
  55.4 0.0 collective-permute-done
  55.4 0.0 collective-permute-done.1
  55.4 0.0 collective-permute-done.2
  55.4 0.0 collective-permute-done.3
  55.4 2.4 %fusion.15 = f32[512,64]{0,1:T(8,128)S(1)} fusion(bf16[1,2,512,2048]{3,2,1,0:T(8,128)(2,1)} %param.10, s32[]{:T(128)S(6)} %select_n.47, bf16[1,2048,64]{1,2,0:T(8,128)(2,1)S(1)} %bitcast.48, bf16[1,2048,64]{1,2,0:T(8,128)(2,1)S(1)} %bitcast.49, bf16[1,2048,64]{1,2,0:T(8,128)(2,1)S(1)} %bitcast.50, bf16[1,2048,64]{1,2,0:T(8,128)(2,1)S(1)} %bitcast.51, ...), kind=kOutput, calls=%fused_computation.10 | convolution fusion | flops 134643712 | bytes 3277316 | tf_op jit(solution)/shard_map/dot_general | solution.py:37
  57.8 3.0 %fusion.9 = f32[512,64]{0,1:T(8,128)} fusion(f32[512,64]{0,1:T(8,128)S(1)} %convolution_bitcast_fusion, f32[512,64]{0,1:T(8,128)S(1)} %fusion.15, bf16[2048,64]{0,1:T(8,128)(2,1)S(1)} %all_gather.6, bf16[1,2,512,2048]{3,2,1,0:T(8,128)(2,1)} %param.10), kind=kOutput, calls=%fused_computation.8 | convolution fusion | flops 134283264 | bytes 2752512 | tf_op jit(solution)/shard_map/dot_general | solution.py:36
  (2 shorter events, 0.0 us)
Async XLA Ops:
  0.0 55.2 %copy-start = (bf16[512,64]{0,1:T(8,128)(2,1)S(1)}, bf16[512,64]{0,1:T(8,128)(2,1)}, u32[]{:S(2)}) copy-start(bf16[512,64]{0,1:T(8,128)(2,1)} %param.16) | copy-start | bytes 196612
  8.2 47.2 %collective-permute-start = (bf16[2048,64]{0,1:T(8,128)(2,1)S(1)}, bf16[2048,64]{0,1:T(8,128)(2,1)S(1)}, u32[]{:S(2)}, u32[]{:S(2)}) collective-permute-start(bf16[2048,64]{0,1:T(8,128)(2,1)S(1)} %all_gather.6), channel_id=1, source_target_pairs={{0,8},{4,12},{1,9},{5,13},{2,10},{6,14},{3,11},{7,15},{16,24},{20,... | collective-permute-start | bytes 786440 | tf_op jit(solution)/shard_map/ppermute | solution.py:10
  12.7 42.7 %collective-permute-start.1 = (bf16[2048,64]{0,1:T(8,128)(2,1)S(1)}, bf16[2048,64]{0,1:T(8,128)(2,1)S(1)}, u32[]{:S(2)}, u32[]{:S(2)}) collective-permute-start(bf16[2048,64]{0,1:T(8,128)(2,1)S(1)} %all_gather.6), channel_id=1, source_target_pairs={{0,4},{4,8},{8,12},{1,5},{5,9},{9,13},{2,6},{6,10},{10,14},{3,7},{... | collective-permute-start | bytes 786440 | tf_op jit(solution)/shard_map/ppermute | solution.py:10
  16.2 39.2 %collective-permute-start.2 = (bf16[2048,64]{0,1:T(8,128)(2,1)S(1)}, bf16[2048,64]{0,1:T(8,128)(2,1)S(1)}, u32[]{:S(2)}, u32[]{:S(2)}) collective-permute-start(bf16[2048,64]{0,1:T(8,128)(2,1)S(1)} %all_gather.6), channel_id=1, source_target_pairs={{4,0},{8,4},{12,8},{5,1},{9,5},{13,9},{6,2},{10,6},{14,10},{7,3},{... | collective-permute-start | bytes 786440 | tf_op jit(solution)/shard_map/ppermute | solution.py:10
  17.5 37.9 %collective-permute-start.3 = (bf16[2048,64]{0,1:T(8,128)(2,1)S(1)}, bf16[2048,64]{0,1:T(8,128)(2,1)S(1)}, u32[]{:S(2)}, u32[]{:S(2)}) collective-permute-start(bf16[2048,64]{0,1:T(8,128)(2,1)S(1)} %all_gather.6), channel_id=1, source_target_pairs={{8,0},{12,4},{9,1},{13,5},{10,2},{14,6},{11,3},{15,7},{24,16},{28,... | collective-permute-start | bytes 786440 | tf_op jit(solution)/shard_map/ppermute | solution.py:10
where the time goes:
time: 61.3 us; the launch traced here: 60.8 us
  blocking collectives  32.9 us (54%)
  starting transfers between devices  10.6 us (17%)
  matrix products  7.95 us (13%)
  local copies, waits for them, and re-layouts  4.33 us (7%)
  other arithmetic  2.98 us (5%)
  between operations  2.04 us (3%)
    all_gather x1, blocking collectives, body(): table = lax.all_gather(proj[None], 'cell', axis=0, tiled=True)  14.3 us
    psum x1, blocking collectives, body(): proj = lax.psum(partial_proj, 'col')  11.4 us
    ppermute x4, starting transfers between devices, shifted(): return lax.ppermute(value, axis, pairs)  10.6 us
    all_gather x1, blocking collectives, body(): whole = lax.all_gather(rounded, 'col', axis=0, tiled=True)  7.22 us
    dot_general x1, matrix products, body(): own_term = jnp.dot(tiles[0], whole, preferred_element_type=jnp.float32)  3.02 us
    dot_general x1, matrix products, body(): other_term = jnp.dot(tiles[1], beside, preferred_element_type=jnp.float32)  2.35 us
    dot_general x1, matrix products, coupling(): jnp.einsum('kab,kbw->aw', masked, picked, precision=lax.Precision.HIGHEST)  1.42 us
    and x1, other arithmetic, coupling(): picked = jnp.take(table, sources, axis=0)  1.34 us
  transfers between devices with their start and end apart: 4, of which 0 were waited for; matrix products, arithmetic and copies ran while one was open for 15% of the time, Pallas kernels for 0%

commit v1 on v0

v1 whole, which is shorter than its diff:
```python
import functools

import jax
import jax.numpy as jnp
from jax import lax
from jax.experimental import pallas as pl
from jax.experimental.pallas import tpu as pltpu
from jax.sharding import PartitionSpec as P

REACH = 2
F32 = jnp.float32
BF16 = jnp.bfloat16
VMEM = pl.BlockSpec(memory_space=pltpu.VMEM)
SMEM = pl.BlockSpec(memory_space=pltpu.SMEM)
ANY = pl.BlockSpec(memory_space=pl.ANY)
NT = (((1,), (1,)), ((), ()))


def call(kernel, out, inputs, specs, scratch=(), flops=0, moved=0, name=None):
    return pl.pallas_call(
        kernel,
        out_shape=out,
        in_specs=specs,
        out_specs=jax.tree.map(lambda _: VMEM, out),
        scratch_shapes=list(scratch),
        cost_estimate=pl.CostEstimate(flops=flops, bytes_accessed=moved, transcendentals=0),
        compiler_params=pltpu.CompilerParams(vmem_limit_bytes=16 << 20),
        name=name,
    )(*inputs)


def split(value):
    high = value.astype(BF16)
    low = (value - high.astype(F32)).astype(BF16)
    return high, low


def join(ref, at, width):
    high = ref[:, at : at + width].astype(F32)
    return high + ref[:, at + width : at + 2 * width].astype(F32)


def first_kernel(grad_ref, basis_ref, out_ref):
    rank, rows = basis_ref.shape
    rounded = grad_ref[...].astype(BF16)
    out_ref[:, :rows] = rounded
    partial = lax.dot_general(rounded, basis_ref[...], NT, preferred_element_type=F32)
    high, low = split(partial)
    out_ref[:, rows : rows + rank] = high
    out_ref[:, rows + rank :] = low


def table_kernel(count_ref, offset_ref, source_ref, far_ref, cores_ref, mix_ref, flag_ref):
    owner = lax.axis_index("cell")
    slots, rank, _ = cores_ref.shape
    cells = mix_ref.shape[1] // rank
    used = far_ref[owner]
    for step in range(cells):
        total = jnp.zeros((rank, rank), F32)
        for slot in range(slots):
            hit = jnp.logical_and(source_ref[owner, slot] == (owner ^ step), slot < used)
            total = total + jnp.where(hit, cores_ref[slot], 0.0)
        mix_ref[:, step * rank : (step + 1) * rank] = total
    beyond = owner ^ 2
    asked = beyond + offset_ref[beyond] == owner ^ 1
    beside = offset_ref[owner] + owner == owner ^ 1
    double = count_ref[owner] == 2
    for row, value in enumerate((asked, beside, double)):
        flag_ref[row] = jnp.full(flag_ref.shape[1:], value.astype(F32), F32)


def pick(flag_ref, row, yes, no):
    shape = yes.shape
    mask = jnp.broadcast_to(flag_ref[row][:1, :1], shape) > 0.5
    return jnp.where(mask, yes.astype(F32), no.astype(F32)).astype(BF16)


def second_kernel(flag_ref, mine_ref, near_ref, out_ref, *, rows):
    out_ref[:, :rows] = pick(flag_ref, 0, near_ref[:, :rows], mine_ref[:, :rows])
    tail = mine_ref.shape[1] - rows
    out_ref[:, rows : rows + tail] = mine_ref[:, rows:]
    out_ref[:, rows + tail :] = near_ref[:, rows:]


def third_kernel(flag_ref, mix_ref, mine_ref, near_ref, far_ref, out_ref, *, rows):
    rank = mix_ref.shape[0]
    beside = pick(flag_ref, 1, near_ref[:, :rows], far_ref[:, :rows])
    beside = pick(flag_ref, 2, beside, jnp.zeros_like(beside))
    out_ref[:, :rows] = mine_ref[:, :rows]
    out_ref[:, rows : 2 * rows] = beside
    table = jnp.concatenate(
        (
            join(mine_ref, rows, rank),
            join(near_ref, rows, rank),
            join(far_ref, rows, rank),
            join(far_ref, rows + 2 * rank, rank),
        ),
        axis=1,
    )
    core = lax.dot_general(
        table, mix_ref[...], NT, precision=lax.Precision.HIGHEST, preferred_element_type=F32
    )
    high, low = split(core)
    out_ref[:, 2 * rows : 2 * rows + rank] = high
    out_ref[:, 2 * rows + rank :] = low


def widen_kernel(mine_ref, other_ref, out_ref, *, rank):
    body = mine_ref.shape[1] - 2 * rank
    out_ref[:, :body] = mine_ref[:, :body]
    out_ref[:, body : 2 * body] = other_ref[:, :body]
    high, low = split(join(mine_ref, body, rank) + join(other_ref, body, rank))
    out_ref[:, 2 * body : 2 * body + rank] = high
    out_ref[:, 2 * body + rank :] = low


def last_kernel(mine_ref, other_ref, basis_ref, tiles_ref, out_ref, buffer, sems, *, order):
    place = lax.axis_index("col")
    rank, rows = basis_ref.shape
    body = mine_ref.shape[1] - 2 * rank
    copies = []
    for item, (part, spot) in enumerate(order):
        columns = pl.ds(pl.multiple_of((place ^ spot) * rows, rows), rows)
        copy = pltpu.make_async_copy(
            tiles_ref.at[part, :, columns], buffer.at[item], sems.at[item]
        )
        copy.start()
        copies.append(copy)
    core = join(mine_ref, body, rank) + join(other_ref, body, rank)
    total = jnp.dot(core.astype(BF16), basis_ref[...], preferred_element_type=F32)
    half = len(order) // 2
    for item, copy in enumerate(copies):
        copy.wait()
        source = mine_ref if item < half else other_ref
        at = (item % half) * rows
        total = total + lax.dot_general(
            source[:, at : at + rows], buffer[item], NT, preferred_element_type=F32
        )
    out_ref[...] = total


def swap(value, axis, step):
    size = lax.axis_size(axis)
    return lax.ppermute(value, axis, [(i, i ^ step) for i in range(size)])


def shifted(value, axis, by):
    size = lax.axis_size(axis)
    return lax.ppermute(value, axis, [(i, i + by) for i in range(size) if 0 <= i + by < size])


def over_small_chain(first, tables, cores, rows):
    width, length = first.shape
    rank = cores.shape[1]
    near = swap(first, "cell", 1)
    mix, flags = call(
        table_kernel,
        (
            jax.ShapeDtypeStruct((rank, 4 * rank), F32),
            jax.ShapeDtypeStruct((3, 8, 128), F32),
        ),
        (*tables, cores),
        [SMEM] * 4 + [VMEM],
        moved=cores.size * 4,
        name="tables",
    )
    second = call(
        functools.partial(second_kernel, rows=rows),
        jax.ShapeDtypeStruct((width, 2 * length - rows), BF16),
        (flags, first, near),
        [VMEM] * 3,
        moved=4 * first.size,
        name="second",
    )
    far = swap(second, "cell", 2)
    return call(
        functools.partial(third_kernel, rows=rows),
        jax.ShapeDtypeStruct((width, length + rows), BF16),
        (flags, mix, first, near, far),
        [VMEM] * 5,
        moved=8 * first.size,
        name="third",
    )


def over_long_chain(first, tables, cores, rows):
    owner = lax.axis_index("cell")
    rank = cores.shape[1]
    counts, offsets, sources, used = (table[owner] for table in tables)
    steps = [step for step in range(-REACH, REACH + 1) if step]
    moved = jnp.stack([shifted(first[:, :rows], "cell", -step) for step in steps])
    beside = lax.dynamic_index_in_dim(
        moved, offsets + REACH - (offsets > 0).astype(jnp.int32), 0, keepdims=False
    )
    beside = jnp.where(counts == 2, beside, jnp.zeros_like(beside))
    high, low = first[:, rows : rows + rank], first[:, rows + rank :]
    partial = high.astype(F32) + low.astype(F32)
    table = lax.all_gather(partial[None], "cell", axis=0, tiled=True)
    picked = jnp.take(table, sources, axis=0)
    slots = jnp.arange(cores.shape[0], dtype=jnp.int32)
    masked = jnp.where((slots < used)[:, None, None], cores, jnp.zeros_like(cores))
    core = jnp.einsum("kab,kwb->wa", masked, picked, precision=lax.Precision.HIGHEST)
    return jnp.concatenate((first[:, :rows], beside, *split(core)), axis=1)


def body(
    grad, near_tiles, tile_count, near_offset, far_src, far_count, far_cores, basis_out, basis_in
):
    rows, width = grad.shape
    rank = basis_in.shape[1]
    cells, parts = lax.axis_size("cell"), lax.axis_size("col")
    first = call(
        first_kernel,
        jax.ShapeDtypeStruct((width, rows + 2 * rank), BF16),
        (grad.T, basis_in.T),
        [VMEM] * 2,
        moved=8 * grad.size,
        name="first",
    )
    tables = (tile_count, near_offset, far_src, far_count)
    over_cells = over_small_chain if cells == 2 * REACH else over_long_chain
    held = over_cells(first, tables, far_cores[0], rows)
    order = [(0, 0), (1, 0)]
    step = parts // 2
    while step > 1:
        other = swap(held, "col", step)
        held = call(
            functools.partial(widen_kernel, rank=rank),
            jax.ShapeDtypeStruct((width, 2 * held.shape[1] - 2 * rank), BF16),
            (held, other),
            [VMEM] * 2,
            moved=8 * held.size,
            name="widen",
        )
        order += [(part, spot ^ step) for part, spot in order]
        step //= 2
    other = swap(held, "col", 1)
    order += [(part, spot ^ 1) for part, spot in order]
    out = call(
        functools.partial(last_kernel, order=order),
        jax.ShapeDtypeStruct((width, rows), F32),
        (held, other, basis_out.T, near_tiles[0]),
        [VMEM] * 3 + [ANY],
        scratch=(
            pltpu.VMEM((len(order), rows, rows), BF16),
            pltpu.SemaphoreType.DMA((len(order),)),
        ),
        flops=2 * near_tiles.size * width,
        moved=2 * near_tiles.size,
        name="last",
    )
    return out.T


def solution(mesh):
    placed = (
        P(("chain", "cell", "col"), None),
        P("cell", None, "col", None),
        P(),
        P(),
        P(),
        P(),
        P("cell", None, None, None),
        P(("cell", "col"), None),
        P(("cell", "col"), None),
    )
    return jax.shard_map(
        body,
        mesh=mesh,
        in_specs=placed,
        out_specs=P(("chain", "cell", "col"), None),
        check_vma=False,
    )
```

time: 61.3 us -> 30.8 us (0.50)
  blocking collectives: 32.9 us -> 0 us
  waiting for transfers between devices: 0.01 us -> 10.3 us
  matrix products: 7.95 us -> 0 us
  Pallas kernels: 0 us -> 4.49 us
  local copies, waits for them, and re-layouts: 4.33 us -> 8.36 us
  starting transfers between devices: 10.6 us -> 7.3 us
  other arithmetic: 2.98 us -> 0 us
  between operations: 2.04 us -> 0.04 us
    all_gather x2 -> x0, blocking collectives: 21.5 us -> none  [the longest x1 14.3 us: body(): table = lax.all_gather(proj[None], 'cell', axis=0, tiled=True)]
    psum x1 -> x0, blocking collectives: 11.4 us -> none  [body(): proj = lax.psum(partial_proj, 'col')]
    ppermute x4, waiting for transfers between devices: 0.01 us -> 10.3 us  [swap(): return lax.ppermute(value, axis, [(i, i ^ step) for i in range(size)])]
    unnamed x2 -> x18, local copies, waits for them, and re-layouts: 0.01 us -> 8.36 us
    dot_general x5 -> x0, matrix products: 7.95 us -> none  [the longest x1 3.02 us: body(): own_term = jnp.dot(tiles[0], whole, preferred_element_type=jnp.float32)]
    pallas_call x0 -> x6, Pallas kernels: none -> 4.49 us  [call(): pl.pallas_call(kernel, out_shape=out, in_specs=specs, out_specs=jax.tree....]
    dynamic_slice x3 -> x0, local copies, waits for them, and re-layouts: 3.76 us -> none  [the longest x1 1.27 us: body(): tile_count[owner] == 2]
    ppermute x4, starting transfers between devices: 10.6 us -> 7.3 us  [swap(): return lax.ppermute(value, axis, [(i, i ^ step) for i in range(size)])]
  transfers between devices with their start and end apart: 4 -> 4, of which waited for: 0 -> 3; matrix products, arithmetic and copies ran while one was open for 15% -> 0% of each run, Pallas kernels for 0% -> 2%
where the time goes in v1:
time: 30.8 us; the launch traced here: 30.5 us
  waiting for transfers between devices  10.3 us (33%)
  local copies, waits for them, and re-layouts  8.36 us (27%)
  starting transfers between devices  7.3 us (24%)
  Pallas kernels  4.49 us (15%)
    ppermute x4, waiting for transfers between devices, swap(): return lax.ppermute(value, axis, [(i, i ^ step) for i in range(size)])  10.3 us
    unnamed x18, local copies, waits for them, and re-layouts  8.36 us
    ppermute x4, starting transfers between devices, swap(): return lax.ppermute(value, axis, [(i, i ^ step) for i in range(size)])  7.3 us
    pallas_call x6, Pallas kernels, call(): pl.pallas_call(kernel, out_shape=out, in_specs=specs, out_specs=jax.tree....  4.49 us
  transfers between devices with their start and end apart: 4, of which 3 were waited for; matrix products, arithmetic and copies ran while one was open for 0% of the time, Pallas kernels for 2%

profile of v1, /device:TPU:0, one launch (start us, length us, event | category | flops | bytes accessed | tf_op | source)
XLA Modules:
  0.0 30.5 jit_solution(5162879828854870328)
XLA Ops:
  0.0 0.0 copy-start.2
  0.0 0.9 %copy-done.2 = f32[512,64]{0,1:T(8,128)S(1)} copy-done((f32[512,64]{0,1:T(8,128)S(1)}, f32[512,64]{0,1:T(8,128)}, u32[]{:S(2)}) %copy-start.2) | copy-done | bytes 131096
  0.9 0.0 copy-start.4
  0.9 0.8 %copy-done.4 = bf16[512,64]{0,1:T(8,128)(2,1)S(1)} copy-done((bf16[512,64]{0,1:T(8,128)(2,1)S(1)}, bf16[512,64]{0,1:T(8,128)(2,1)}, u32[]{:S(2)}) %copy-start.4) | copy-done | bytes 65560
  1.7 0.2 first.1.mine_ref
  2.0 3.1 %collective-permute-start = (bf16[64,640]{1,0:T(8,128)(2,1)S(1)}, bf16[64,640]{1,0:T(8,128)(2,1)S(1)}, u32[]{:S(2)}, u32[]{:S(2)}) collective-permute-start(bf16[64,640]{1,0:T(8,128)(2,1)S(1)} %first.1.mine_ref), channel_id=1, source_target_pairs={{0,4},{4,0},{8,12},{12,8},{1,5},{5,1},{9,13},{13,9},{2,6},{6,2},{1... | collective-permute-start | bytes 245768 | tf_op jit(solution)/shard_map/ppermute | solution.py:144
  5.0 0.9 %copy-done.1 = f32[1,8,64,64]{3,2,1,0:T(8,128)S(1)} copy-done((f32[1,8,64,64]{3,2,1,0:T(8,128)S(1)}, f32[1,8,64,64]{3,2,1,0:T(8,128)}, u32[]{:S(2)}) %copy-start.1) | copy-done | bytes 131096
  6.0 0.7 %copy-done.5 = s32[4,8]{1,0:T(4,128)S(1)} copy-done((s32[4,8]{1,0:T(4,128)S(1)}, s32[4,8]{1,0:T(4,128)}, u32[]{:S(2)}) %copy-start.5) | copy-done | bytes 152
  6.7 0.7 %copy-done.6 = s32[4]{0:T(128)S(1)} copy-done((s32[4]{0:T(128)S(1)}, s32[4]{0:T(128)}, u32[]{:S(2)}) %copy-start.6) | copy-done | bytes 40
  7.3 0.7 %copy-done.7 = s32[4]{0:T(128)S(1)} copy-done((s32[4]{0:T(128)S(1)}, s32[4]{0:T(128)}, u32[]{:S(2)}) %copy-start.7) | copy-done | bytes 40
  8.0 0.7 %copy-done.8 = s32[4]{0:T(128)S(1)} copy-done((s32[4]{0:T(128)S(1)}, s32[4]{0:T(128)}, u32[]{:S(2)}) %copy-start.8) | copy-done | bytes 40
  8.6 0.7 %tables.1 = (f32[64,256]{1,0:T(8,128)S(1)}, f32[3,8,128]{2,1,0:T(8,128)S(1)}) custom-call(s32[4]{0:T(128)S(1)} %copy-done.6, s32[4]{0:T(128)S(1)} %copy-done.7, s32[4,8]{1,0:T(4,128)S(1)} %copy-done.5, s32[4]{0:T(128)S(1)} %copy-done.8, f32[8,64,64]{2,1,0:T(8,128)S(1)} %bitcast.7), custom_call_target="tpu_custom_call" | custom-call | bytes 131072 | tf_op jit(solution)/shard_map/tables/pallas_call | solution.py:20
  9.3 0.0 collective-permute-done.near_ref
  9.4 2.6 %collective-permute-start.1 = (bf16[64,768]{1,0:T(8,128)(2,1)S(1)}, bf16[64,768]{1,0:T(8,128)(2,1)S(1)}, u32[]{:S(2)}, u32[]{:S(2)}) collective-permute-start(bf16[64,768]{1,0:T(8,128)(2,1)S(1)} %second.1), channel_id=1, source_target_pairs={{0,8},{4,12},{8,0},{12,4},{1,9},{5,13},{9,1},{13,5},{2,10},{6,14},... | collective-permute-start | bytes 294920 | tf_op jit(solution)/shard_map/ppermute | solution.py:144
  12.1 4.5 %collective-permute-done.1.far_ref = bf16[64,768]{1,0:T(8,128)(2,1)S(1)} collective-permute-done((bf16[64,768]{1,0:T(8,128)(2,1)S(1)}, bf16[64,768]{1,0:T(8,128)(2,1)S(1)}, u32[]{:S(2)}, u32[]{:S(2)}) %collective-permute-start.1) | collective-permute-done | bytes 98336 | tf_op jit(solution)/shard_map/ppermute | solution.py:144
  16.6 0.4 %third.1.mine_ref = bf16[64,1152]{1,0:T(8,128)(2,1)S(1)} custom-call(f32[3,8,128]{2,1,0:T(8,128)S(1)} %get-tuple-element.7.flag_ref, f32[64,256]{1,0:T(8,128)S(1)} %get-tuple-element.8.mix_ref, bf16[64,640]{1,0:T(8,128)(2,1)S(1)} %first.1.mine_ref, bf16[64,640]{1,0:T(8,128)(2,1)S(1)} %collective-permute-done.near_ref, ...), custom_call_target="tpu_custom_call" | custom-call | bytes 327680 | tf_op jit(solution)/shard_map/third/pallas_call | solution.py:20
  17.0 1.6 %collective-permute-start.2 = (bf16[64,1152]{1,0:T(8,128)(2,1)S(1)}, bf16[64,1152]{1,0:T(8,128)(2,1)S(1)}, u32[]{:S(2)}, u32[]{:S(2)}) collective-permute-start(bf16[64,1152]{1,0:T(8,128)(2,1)S(1)} %third.1.mine_ref), channel_id=1, source_target_pairs={{0,2},{1,3},{2,0},{3,1},{4,6},{5,7},{6,4},{7,5},{8,10},{9,11},{10,... | collective-permute-start | bytes 442376 | tf_op jit(solution)/shard_map/ppermute | solution.py:144
  18.5 4.2 %collective-permute-done.2.other_ref = bf16[64,1152]{1,0:T(8,128)(2,1)S(1)} collective-permute-done((bf16[64,1152]{1,0:T(8,128)(2,1)S(1)}, bf16[64,1152]{1,0:T(8,128)(2,1)S(1)}, u32[]{:S(2)}, u32[]{:S(2)}) %collective-permute-start.2) | collective-permute-done | bytes 147488 | tf_op jit(solution)/shard_map/ppermute | solution.py:144
  22.8 0.2 widen.1.mine_ref
  22.9 0.0 collective-permute-start.3
  22.9 1.5 %collective-permute-done.3.other_ref = bf16[64,2176]{1,0:T(8,128)(2,1)S(1)} collective-permute-done((bf16[64,2176]{1,0:T(8,128)(2,1)S(1)}, bf16[64,2176]{1,0:T(8,128)(2,1)S(1)}, u32[]{:S(2)}, u32[]{:S(2)}) %collective-permute-start.3) | collective-permute-done | bytes 278560 | tf_op jit(solution)/shard_map/ppermute | solution.py:144
  24.5 2.2 %copy-done = bf16[1,2,512,2048]{3,2,1,0:T(8,128)(2,1)S(1)} copy-done((bf16[1,2,512,2048]{3,2,1,0:T(8,128)(2,1)S(1)}, bf16[1,2,512,2048]{3,2,1,0:T(8,128)(2,1)}, u32[]{:S(2)}) %copy-start) | copy-done | bytes 4194328
  26.7 0.8 %copy-done.3 = bf16[512,64]{0,1:T(8,128)(2,1)S(1)} copy-done((bf16[512,64]{0,1:T(8,128)(2,1)S(1)}, bf16[512,64]{0,1:T(8,128)(2,1)}, u32[]{:S(2)}) %copy-start.3) | copy-done | bytes 65560
  27.5 3.0 %last.1 = f32[64,512]{1,0:T(8,128)} custom-call(bf16[64,2176]{1,0:T(8,128)(2,1)S(1)} %widen.1.mine_ref, bf16[64,2176]{1,0:T(8,128)(2,1)S(1)} %collective-permute-done.3.other_ref, bf16[64,512]{1,0:T(8,128)(2,1)S(1)} %bitcast.9, bf16[2,512,2048]{2,1,0:T(8,128)(2,1)S(1)} %bitcast.6), custom_call_target="tpu_custom_call" | custom-call | flops 268435456 | bytes 4194304 | tf_op jit(solution)/shard_map/last/pallas_call | solution.py:20
  (8 shorter events, 0.1 us)
Async XLA Ops:
  0.0 0.9 %copy-start.2 = (f32[512,64]{0,1:T(8,128)S(1)}, f32[512,64]{0,1:T(8,128)}, u32[]{:S(2)}) copy-start(f32[512,64]{0,1:T(8,128)} %param.9) | copy-start | bytes 393220
  0.9 0.8 %copy-start.4 = (bf16[512,64]{0,1:T(8,128)(2,1)S(1)}, bf16[512,64]{0,1:T(8,128)(2,1)}, u32[]{:S(2)}) copy-start(bf16[512,64]{0,1:T(8,128)(2,1)} %param.17) | copy-start | bytes 196612
  2.0 7.4 %collective-permute-start = (bf16[64,640]{1,0:T(8,128)(2,1)S(1)}, bf16[64,640]{1,0:T(8,128)(2,1)S(1)}, u32[]{:S(2)}, u32[]{:S(2)}) collective-permute-start(bf16[64,640]{1,0:T(8,128)(2,1)S(1)} %first.1.mine_ref), channel_id=1, source_target_pairs={{0,4},{4,0},{8,12},{12,8},{1,5},{5,1},{9,13},{13,9},{2,6},{6,2},{1... | collective-permute-start | bytes 245768 | tf_op jit(solution)/shard_map/ppermute | solution.py:144
  5.0 0.9 %copy-start.1 = (f32[1,8,64,64]{3,2,1,0:T(8,128)S(1)}, f32[1,8,64,64]{3,2,1,0:T(8,128)}, u32[]{:S(2)}) copy-start(f32[1,8,64,64]{3,2,1,0:T(8,128)} %param.15) | copy-start | bytes 393220
  6.0 0.7 %copy-start.5 = (s32[4,8]{1,0:T(4,128)S(1)}, s32[4,8]{1,0:T(4,128)}, u32[]{:S(2)}) copy-start(s32[4,8]{1,0:T(4,128)} %source_ref.1) | copy-start | bytes 388
  6.7 0.7 %copy-start.6 = (s32[4]{0:T(128)S(1)}, s32[4]{0:T(128)}, u32[]{:S(2)}) copy-start(s32[4]{0:T(128)} %count_ref.1) | copy-start | bytes 52
  7.3 0.7 %copy-start.7 = (s32[4]{0:T(128)S(1)}, s32[4]{0:T(128)}, u32[]{:S(2)}) copy-start(s32[4]{0:T(128)} %offset_ref.1) | copy-start | bytes 52
  8.0 0.7 %copy-start.8 = (s32[4]{0:T(128)S(1)}, s32[4]{0:T(128)}, u32[]{:S(2)}) copy-start(s32[4]{0:T(128)} %far_ref.1) | copy-start | bytes 52
  9.4 7.2 %collective-permute-start.1 = (bf16[64,768]{1,0:T(8,128)(2,1)S(1)}, bf16[64,768]{1,0:T(8,128)(2,1)S(1)}, u32[]{:S(2)}, u32[]{:S(2)}) collective-permute-start(bf16[64,768]{1,0:T(8,128)(2,1)S(1)} %second.1), channel_id=1, source_target_pairs={{0,8},{4,12},{8,0},{12,4},{1,9},{5,13},{9,1},{13,5},{2,10},{6,14},... | collective-permute-start | bytes 294920 | tf_op jit(solution)/shard_map/ppermute | solution.py:144
  17.0 5.8 %collective-permute-start.2 = (bf16[64,1152]{1,0:T(8,128)(2,1)S(1)}, bf16[64,1152]{1,0:T(8,128)(2,1)S(1)}, u32[]{:S(2)}, u32[]{:S(2)}) collective-permute-start(bf16[64,1152]{1,0:T(8,128)(2,1)S(1)} %third.1.mine_ref), channel_id=1, source_target_pairs={{0,2},{1,3},{2,0},{3,1},{4,6},{5,7},{6,4},{7,5},{8,10},{9,11},{10,... | collective-permute-start | bytes 442376 | tf_op jit(solution)/shard_map/ppermute | solution.py:144
  22.9 1.6 %collective-permute-start.3 = (bf16[64,2176]{1,0:T(8,128)(2,1)S(1)}, bf16[64,2176]{1,0:T(8,128)(2,1)S(1)}, u32[]{:S(2)}, u32[]{:S(2)}) collective-permute-start(bf16[64,2176]{1,0:T(8,128)(2,1)S(1)} %widen.1.mine_ref), channel_id=1, source_target_pairs={{0,1},{1,0},{2,3},{3,2},{4,5},{5,4},{6,7},{7,6},{8,9},{9,8},{10,11... | collective-permute-start | bytes 835592 | tf_op jit(solution)/shard_map/ppermute | solution.py:144
  24.5 2.2 %copy-start = (bf16[1,2,512,2048]{3,2,1,0:T(8,128)(2,1)S(1)}, bf16[1,2,512,2048]{3,2,1,0:T(8,128)(2,1)}, u32[]{:S(2)}) copy-start(bf16[1,2,512,2048]{3,2,1,0:T(8,128)(2,1)} %param.10) | copy-start | bytes 12582916
  26.7 0.8 %copy-start.3 = (bf16[512,64]{0,1:T(8,128)(2,1)S(1)}, bf16[512,64]{0,1:T(8,128)(2,1)}, u32[]{:S(2)}) copy-start(bf16[512,64]{0,1:T(8,128)(2,1)} %param.16) | copy-start | bytes 196612

commit v2 on v1

--- a/solution.py
+++ b/solution.py
@@ -11,12 +11,15 @@
 F32 = jnp.float32
 BF16 = jnp.bfloat16
 VMEM = pl.BlockSpec(memory_space=pltpu.VMEM)
-SMEM = pl.BlockSpec(memory_space=pltpu.SMEM)
-ANY = pl.BlockSpec(memory_space=pl.ANY)
+HBM = pl.BlockSpec(memory_space=pltpu.HBM)
 NT = (((1,), (1,)), ((), ()))
 
 
 def call(kernel, out, inputs, specs, scratch=(), flops=0, moved=0, name=None):
+    inputs = [
+        pltpu.with_memory_space_constraint(value, pltpu.HBM) if spec is HBM else value
+        for value, spec in zip(inputs, specs)
+    ]
     return pl.pallas_call(
         kernel,
         out_shape=out,
@@ -40,19 +43,36 @@
     return high + ref[:, at + width : at + 2 * width].astype(F32)
 
 
-def first_kernel(grad_ref, basis_ref, out_ref):
+def fetch(sources, targets, sems):
+    copies = [
+        pltpu.make_async_copy(source, target, sems.at[index])
+        for index, (source, target) in enumerate(zip(sources, targets))
+    ]
+    for copy in copies:
+        copy.start()
+    return copies
+
+
+def first_kernel(grad_hbm, basis_hbm, out_ref, grad_ref, basis_ref, sems):
     rank, rows = basis_ref.shape
+    copies = fetch((grad_hbm, basis_hbm), (grad_ref, basis_ref), sems)
+    copies[0].wait()
     rounded = grad_ref[...].astype(BF16)
     out_ref[:, :rows] = rounded
+    copies[1].wait()
     partial = lax.dot_general(rounded, basis_ref[...], NT, preferred_element_type=F32)
     high, low = split(partial)
     out_ref[:, rows : rows + rank] = high
     out_ref[:, rows + rank :] = low
 
 
-def table_kernel(count_ref, offset_ref, source_ref, far_ref, cores_ref, mix_ref, flag_ref):
+def table_kernel(*refs):
+    inputs, (mix_ref, flag_ref), held, sems = refs[:5], refs[5:7], refs[7:12], refs[12]
+    count_ref, offset_ref, source_ref, far_ref, cores_ref = held
     owner = lax.axis_index("cell")
     slots, rank, _ = cores_ref.shape
+    for copy in fetch(inputs, held, sems):
+        copy.wait()
     cells = mix_ref.shape[1] // rank
     used = far_ref[owner]
     for step in range(cells):
@@ -105,7 +125,8 @@
     out_ref[:, 2 * rows + rank :] = low
 
 
-def widen_kernel(mine_ref, other_ref, out_ref, *, rank):
+def widen_kernel(after_ref, mine_ref, other_ref, out_ref, *, rank):
+    del after_ref
     body = mine_ref.shape[1] - 2 * rank
     out_ref[:, :body] = mine_ref[:, :body]
     out_ref[:, body : 2 * body] = other_ref[:, :body]
@@ -114,29 +135,39 @@
     out_ref[:, 2 * body + rank :] = low
 
 
-def last_kernel(mine_ref, other_ref, basis_ref, tiles_ref, out_ref, buffer, sems, *, order):
+def stage_kernel(after_ref, tiles_hbm, basis_hbm, tiles_ref, basis_ref, sems):
+    del after_ref
+    parts = tiles_ref.shape[0]
+    sources = [tiles_hbm.at[part] for part in range(parts)] + [basis_hbm]
+    targets = [tiles_ref.at[part] for part in range(parts)] + [basis_ref]
+    for copy in fetch(sources, targets, sems):
+        copy.wait()
+
+
+def near(total, held_ref, tiles_ref, order):
     place = lax.axis_index("col")
-    rank, rows = basis_ref.shape
-    body = mine_ref.shape[1] - 2 * rank
-    copies = []
+    rows = tiles_ref.shape[1]
     for item, (part, spot) in enumerate(order):
         columns = pl.ds(pl.multiple_of((place ^ spot) * rows, rows), rows)
-        copy = pltpu.make_async_copy(
-            tiles_ref.at[part, :, columns], buffer.at[item], sems.at[item]
+        total = total + lax.dot_general(
+            held_ref[:, item * rows : (item + 1) * rows],
+            tiles_ref[part, :, columns],
+            NT,
+            preferred_element_type=F32,
         )
-        copy.start()
-        copies.append(copy)
+    return total
+
+
+def near_kernel(mine_ref, tiles_ref, out_ref, *, order):
+    out_ref[...] = near(jnp.zeros(out_ref.shape, F32), mine_ref, tiles_ref, order)
+
+
+def last_kernel(sum_ref, mine_ref, other_ref, basis_ref, tiles_ref, out_ref, *, order):
+    rank = basis_ref.shape[0]
+    body = mine_ref.shape[1] - 2 * rank
     core = join(mine_ref, body, rank) + join(other_ref, body, rank)
-    total = jnp.dot(core.astype(BF16), basis_ref[...], preferred_element_type=F32)
-    half = len(order) // 2
-    for item, copy in enumerate(copies):
-        copy.wait()
-        source = mine_ref if item < half else other_ref
-        at = (item % half) * rows
-        total = total + lax.dot_general(
-            source[:, at : at + rows], buffer[item], NT, preferred_element_type=F32
-        )
-    out_ref[...] = total
+    far = jnp.dot(core.astype(BF16), basis_ref[...], preferred_element_type=F32)
+    out_ref[...] = near(sum_ref[...] + far, other_ref, tiles_ref, order)
 
 
 def swap(value, axis, step):
@@ -152,7 +183,7 @@
 def over_small_chain(first, tables, cores, rows):
     width, length = first.shape
     rank = cores.shape[1]
-    near = swap(first, "cell", 1)
+    beyond = swap(first, "cell", 1)
     mix, flags = call(
         table_kernel,
         (
@@ -160,14 +191,19 @@
             jax.ShapeDtypeStruct((3, 8, 128), F32),
         ),
         (*tables, cores),
-        [SMEM] * 4 + [VMEM],
+        [HBM] * 5,
+        scratch=[
+            *(pltpu.SMEM(table.shape, table.dtype) for table in tables),
+            pltpu.VMEM(cores.shape, cores.dtype),
+            pltpu.SemaphoreType.DMA((5,)),
+        ],
         moved=cores.size * 4,
         name="tables",
     )
     second = call(
         functools.partial(second_kernel, rows=rows),
         jax.ShapeDtypeStruct((width, 2 * length - rows), BF16),
-        (flags, first, near),
+        (flags, first, beyond),
         [VMEM] * 3,
         moved=4 * first.size,
         name="second",
@@ -176,7 +212,7 @@
     return call(
         functools.partial(third_kernel, rows=rows),
         jax.ShapeDtypeStruct((width, length + rows), BF16),
-        (flags, mix, first, near, far),
+        (flags, mix, first, beyond, far),
         [VMEM] * 5,
         moved=8 * first.size,
         name="third",
@@ -213,13 +249,30 @@
         first_kernel,
         jax.ShapeDtypeStruct((width, rows + 2 * rank), BF16),
         (grad.T, basis_in.T),
-        [VMEM] * 2,
+        [HBM] * 2,
+        scratch=[
+            pltpu.VMEM((width, rows), grad.dtype),
+            pltpu.VMEM((rank, rows), basis_in.dtype),
+            pltpu.SemaphoreType.DMA((2,)),
+        ],
         moved=8 * grad.size,
         name="first",
     )
     tables = (tile_count, near_offset, far_src, far_count)
     over_cells = over_small_chain if cells == 2 * REACH else over_long_chain
     held = over_cells(first, tables, far_cores[0], rows)
+    tiles, basis = call(
+        stage_kernel,
+        (
+            jax.ShapeDtypeStruct(near_tiles.shape[1:], near_tiles.dtype),
+            jax.ShapeDtypeStruct((rank, rows), basis_out.dtype),
+        ),
+        (held, near_tiles[0], basis_out.T),
+        [VMEM, HBM, HBM],
+        scratch=[pltpu.SemaphoreType.DMA((near_tiles.shape[1] + 1,))],
+        moved=2 * near_tiles.size,
+        name="stage",
+    )
     order = [(0, 0), (1, 0)]
     step = parts // 2
     while step > 1:
@@ -227,26 +280,30 @@
         held = call(
             functools.partial(widen_kernel, rank=rank),
             jax.ShapeDtypeStruct((width, 2 * held.shape[1] - 2 * rank), BF16),
-            (held, other),
-            [VMEM] * 2,
+            (basis, held, other),
+            [VMEM] * 3,
             moved=8 * held.size,
             name="widen",
         )
         order += [(part, spot ^ step) for part, spot in order]
         step //= 2
     other = swap(held, "col", 1)
-    order += [(part, spot ^ 1) for part, spot in order]
+    total = call(
+        functools.partial(near_kernel, order=order),
+        jax.ShapeDtypeStruct((width, rows), F32),
+        (held, tiles),
+        [VMEM] * 2,
+        flops=tiles.size * width,
+        moved=tiles.size,
+        name="near",
+    )
     out = call(
-        functools.partial(last_kernel, order=order),
+        functools.partial(last_kernel, order=[(part, spot ^ 1) for part, spot in order]),
         jax.ShapeDtypeStruct((width, rows), F32),
-        (held, other, basis_out.T, near_tiles[0]),
-        [VMEM] * 3 + [ANY],
-        scratch=(
-            pltpu.VMEM((len(order), rows, rows), BF16),
-            pltpu.SemaphoreType.DMA((len(order),)),
-        ),
-        flops=2 * near_tiles.size * width,
-        moved=2 * near_tiles.size,
+        (total, held, other, basis, tiles),
+        [VMEM] * 5,
+        flops=tiles.size * width,
+        moved=tiles.size,
         name="last",
     )
     return out.T

time: 30.8 us -> 21.7 us (0.70)
  local copies, waits for them, and re-layouts: 8.36 us -> 0 us
  waiting for transfers between devices: 10.3 us -> 6.32 us
  Pallas kernels: 4.49 us -> 7.38 us
  starting transfers between devices: 7.3 us -> 7.78 us
    unnamed x18 -> x0, local copies, waits for them, and re-layouts: 8.36 us -> none
    ppermute x4, waiting for transfers between devices: 10.3 us -> 6.32 us  [swap(): return lax.ppermute(value, axis, [(i, i ^ step) for i in range(size)])]
    pallas_call x6 -> x8, Pallas kernels: 4.49 us -> 7.38 us  [call(): pl.pallas_call(kernel, out_shape=out, in_specs=specs, out_specs=jax.tree....]
    ppermute x4, starting transfers between devices: 7.3 us -> 7.78 us  [swap(): return lax.ppermute(value, axis, [(i, i ^ step) for i in range(size)])]
  transfers between devices with their start and end apart: 4 -> 4, of which waited for: 3 -> 4; matrix products, arithmetic and copies ran while one was open for 0% -> 0% of each run, Pallas kernels for 2% -> 19%
where the time goes in v2:
time: 21.7 us; the launch traced here: 21.5 us
  starting transfers between devices  7.78 us (36%)
  Pallas kernels  7.38 us (34%)
  waiting for transfers between devices  6.32 us (29%)
    ppermute x4, starting transfers between devices, swap(): return lax.ppermute(value, axis, [(i, i ^ step) for i in range(size)])  7.78 us
    pallas_call x8, Pallas kernels, call(): pl.pallas_call(kernel, out_shape=out, in_specs=specs, out_specs=jax.tree....  7.38 us
    ppermute x4, waiting for transfers between devices, swap(): return lax.ppermute(value, axis, [(i, i ^ step) for i in range(size)])  6.32 us
  transfers between devices with their start and end apart: 4, of which 4 were waited for; matrix products, arithmetic and copies ran while one was open for 0% of the time, Pallas kernels for 19%

profile of v2, /device:TPU:0, one launch (start us, length us, event | category | flops | bytes accessed | tf_op | source)
XLA Modules:
  0.0 21.5 jit_solution(16988703878553613235)
XLA Ops:
  0.0 1.1 %first.1.mine_ref = bf16[64,640]{1,0:T(8,128)(2,1)S(1)} custom-call(f32[64,512]{1,0:T(8,128)} %bitcast.8, bf16[64,512]{1,0:T(8,128)(2,1)} %bitcast.10), custom_call_target="tpu_custom_call" | custom-call | bytes 262144 | tf_op jit(solution)/shard_map/first/pallas_call | solution.py:23
  1.2 3.1 %collective-permute-start = (bf16[64,640]{1,0:T(8,128)(2,1)S(1)}, bf16[64,640]{1,0:T(8,128)(2,1)S(1)}, u32[]{:S(2)}, u32[]{:S(2)}) collective-permute-start(bf16[64,640]{1,0:T(8,128)(2,1)S(1)} %first.1.mine_ref), channel_id=1, source_target_pairs={{0,4},{4,0},{8,12},{12,8},{1,5},{5,1},{9,13},{13,9},{2,6},{6,2},{1... | collective-permute-start | bytes 245768 | tf_op jit(solution)/shard_map/ppermute | solution.py:175
  4.3 1.1 %tables.1 = (f32[64,256]{1,0:T(8,128)S(1)}, f32[3,8,128]{2,1,0:T(8,128)S(1)}) custom-call(s32[4]{0:T(128)} %refs_0_.1, s32[4]{0:T(128)} %refs_1_.1, s32[4,8]{1,0:T(4,128)} %refs_2_.1, s32[4]{0:T(128)} %refs_3_.1, f32[8,64,64]{2,1,0:T(8,128)} %bitcast.7), custom_call_target="tpu_custom_call" | custom-call | bytes 131072 | tf_op jit(solution)/shard_map/tables/pallas_call | solution.py:23
  5.4 1.3 %collective-permute-done.near_ref = bf16[64,640]{1,0:T(8,128)(2,1)S(1)} collective-permute-done((bf16[64,640]{1,0:T(8,128)(2,1)S(1)}, bf16[64,640]{1,0:T(8,128)(2,1)S(1)}, u32[]{:S(2)}, u32[]{:S(2)}) %collective-permute-start) | collective-permute-done | bytes 81952 | tf_op jit(solution)/shard_map/ppermute | solution.py:175
  6.8 3.1 %collective-permute-start.1 = (bf16[64,768]{1,0:T(8,128)(2,1)S(1)}, bf16[64,768]{1,0:T(8,128)(2,1)S(1)}, u32[]{:S(2)}, u32[]{:S(2)}) collective-permute-start(bf16[64,768]{1,0:T(8,128)(2,1)S(1)} %second.1), channel_id=1, source_target_pairs={{0,8},{4,12},{8,0},{12,4},{1,9},{5,13},{9,1},{13,5},{2,10},{6,14},... | collective-permute-start | bytes 294920 | tf_op jit(solution)/shard_map/ppermute | solution.py:175
  9.8 2.9 %collective-permute-done.1.far_ref = bf16[64,768]{1,0:T(8,128)(2,1)S(1)} collective-permute-done((bf16[64,768]{1,0:T(8,128)(2,1)S(1)}, bf16[64,768]{1,0:T(8,128)(2,1)S(1)}, u32[]{:S(2)}, u32[]{:S(2)}) %collective-permute-start.1) | collective-permute-done | bytes 98336 | tf_op jit(solution)/shard_map/ppermute | solution.py:175
  12.7 0.4 %third.1.after_ref.mine_ref = bf16[64,1152]{1,0:T(8,128)(2,1)S(1)} custom-call(f32[3,8,128]{2,1,0:T(8,128)S(1)} %get-tuple-element.9.flag_ref, f32[64,256]{1,0:T(8,128)S(1)} %get-tuple-element.10.mix_ref, bf16[64,640]{1,0:T(8,128)(2,1)S(1)} %first.1.mine_ref, bf16[64,640]{1,0:T(8,128)(2,1)S(1)} %collective-permute-done.near_ref, ...), custom_call_target="tpu_custom_call" | custom-call | bytes 327680 | tf_op jit(solution)/shard_map/third/pallas_call | solution.py:23
  13.1 1.6 %collective-permute-start.2 = (bf16[64,1152]{1,0:T(8,128)(2,1)S(1)}, bf16[64,1152]{1,0:T(8,128)(2,1)S(1)}, u32[]{:S(2)}, u32[]{:S(2)}) collective-permute-start(bf16[64,1152]{1,0:T(8,128)(2,1)S(1)} %third.1.after_ref.mine_ref), channel_id=1, source_target_pairs={{0,2},{1,3},{2,0},{3,1},{4,6},{5,7},{6,4},{7,5},{8,10},{9,11},{10,... | collective-permute-start | bytes 442376 | tf_op jit(solution)/shard_map/ppermute | solution.py:175
  14.7 2.2 %stage.1 = (bf16[2,512,2048]{2,1,0:T(8,128)(2,1)S(1)}, bf16[64,512]{1,0:T(8,128)(2,1)S(1)}) custom-call(bf16[64,1152]{1,0:T(8,128)(2,1)S(1)} %third.1.after_ref.mine_ref, bf16[2,512,2048]{2,1,0:T(8,128)(2,1)} %bitcast.6, bf16[64,512]{1,0:T(8,128)(2,1)} %bitcast.9), custom_call_target="tpu_custom_call" | custom-call | bytes 4194304 | tf_op jit(solution)/shard_map/stage/pallas_call | solution.py:23
  17.0 1.3 %collective-permute-done.2.other_ref = bf16[64,1152]{1,0:T(8,128)(2,1)S(1)} collective-permute-done((bf16[64,1152]{1,0:T(8,128)(2,1)S(1)}, bf16[64,1152]{1,0:T(8,128)(2,1)S(1)}, u32[]{:S(2)}, u32[]{:S(2)}) %collective-permute-start.2) | collective-permute-done | bytes 147488 | tf_op jit(solution)/shard_map/ppermute | solution.py:175
  18.3 0.2 widen.1.mine_ref
  18.5 0.0 collective-permute-start.3
  18.5 0.8 %near.1.sum_ref = f32[64,512]{1,0:T(8,128)S(1)} custom-call(bf16[64,2176]{1,0:T(8,128)(2,1)S(1)} %widen.1.mine_ref, bf16[2,512,2048]{2,1,0:T(8,128)(2,1)S(1)} %get-tuple-element.12.tiles_ref), custom_call_target="tpu_custom_call" | custom-call | flops 134217728 | bytes 2097152 | tf_op jit(solution)/shard_map/near/pallas_call | solution.py:23
  19.3 0.8 %collective-permute-done.3.other_ref = bf16[64,2176]{1,0:T(8,128)(2,1)S(1)} collective-permute-done((bf16[64,2176]{1,0:T(8,128)(2,1)S(1)}, bf16[64,2176]{1,0:T(8,128)(2,1)S(1)}, u32[]{:S(2)}, u32[]{:S(2)}) %collective-permute-start.3) | collective-permute-done | bytes 278560 | tf_op jit(solution)/shard_map/ppermute | solution.py:175
  20.0 1.5 %last.1 = f32[64,512]{1,0:T(8,128)} custom-call(f32[64,512]{1,0:T(8,128)S(1)} %near.1.sum_ref, bf16[64,2176]{1,0:T(8,128)(2,1)S(1)} %widen.1.mine_ref, bf16[64,2176]{1,0:T(8,128)(2,1)S(1)} %collective-permute-done.3.other_ref, bf16[64,512]{1,0:T(8,128)(2,1)S(1)} %get-tuple-element.11.after_ref.basis_ref, bf16[2,512,2048]{2,1,0:T(8,128)(2,1)S(1)} %get-tuple-element.12.tiles_ref), custom_call_target="tpu_custom_call" | custom-call | flops 134217728 | bytes 2097152 | tf_op jit(solution)/shard_map/last/pallas_call | solution.py:23
  (1 shorter events, 0.0 us)
Async XLA Ops:
  1.2 5.6 %collective-permute-start = (bf16[64,640]{1,0:T(8,128)(2,1)S(1)}, bf16[64,640]{1,0:T(8,128)(2,1)S(1)}, u32[]{:S(2)}, u32[]{:S(2)}) collective-permute-start(bf16[64,640]{1,0:T(8,128)(2,1)S(1)} %first.1.mine_ref), channel_id=1, source_target_pairs={{0,4},{4,0},{8,12},{12,8},{1,5},{5,1},{9,13},{13,9},{2,6},{6,2},{1... | collective-permute-start | bytes 245768 | tf_op jit(solution)/shard_map/ppermute | solution.py:175
  6.8 6.0 %collective-permute-start.1 = (bf16[64,768]{1,0:T(8,128)(2,1)S(1)}, bf16[64,768]{1,0:T(8,128)(2,1)S(1)}, u32[]{:S(2)}, u32[]{:S(2)}) collective-permute-start(bf16[64,768]{1,0:T(8,128)(2,1)S(1)} %second.1), channel_id=1, source_target_pairs={{0,8},{4,12},{8,0},{12,4},{1,9},{5,13},{9,1},{13,5},{2,10},{6,14},... | collective-permute-start | bytes 294920 | tf_op jit(solution)/shard_map/ppermute | solution.py:175
  13.1 5.2 %collective-permute-start.2 = (bf16[64,1152]{1,0:T(8,128)(2,1)S(1)}, bf16[64,1152]{1,0:T(8,128)(2,1)S(1)}, u32[]{:S(2)}, u32[]{:S(2)}) collective-permute-start(bf16[64,1152]{1,0:T(8,128)(2,1)S(1)} %third.1.after_ref.mine_ref), channel_id=1, source_target_pairs={{0,2},{1,3},{2,0},{3,1},{4,6},{5,7},{6,4},{7,5},{8,10},{9,11},{10,... | collective-permute-start | bytes 442376 | tf_op jit(solution)/shard_map/ppermute | solution.py:175
  18.5 1.6 %collective-permute-start.3 = (bf16[64,2176]{1,0:T(8,128)(2,1)S(1)}, bf16[64,2176]{1,0:T(8,128)(2,1)S(1)}, u32[]{:S(2)}, u32[]{:S(2)}) collective-permute-start(bf16[64,2176]{1,0:T(8,128)(2,1)S(1)} %widen.1.mine_ref), channel_id=1, source_target_pairs={{0,1},{1,0},{2,3},{3,2},{4,5},{5,4},{6,7},{7,6},{8,9},{9,8},{10,11... | collective-permute-start | bytes 835592 | tf_op jit(solution)/shard_map/ppermute | solution.py:175

commit v3 on v2

v3 whole, which is shorter than its diff:
```python
import functools

import jax
import jax.numpy as jnp
from jax import lax
from jax.experimental import pallas as pl
from jax.experimental.pallas import tpu as pltpu
from jax.sharding import PartitionSpec as P


REACH = 2
F32 = jnp.float32
BF16 = jnp.bfloat16
VMEM = pl.BlockSpec(memory_space=pltpu.VMEM)
HBM = pl.BlockSpec(memory_space=pltpu.HBM)
NT = (((1,), (1,)), ((), ()))


def call(kernel, out, inputs, specs, home=VMEM, scratch=(), flops=0, moved=0):
    inputs = [
        pltpu.with_memory_space_constraint(value, pltpu.HBM) if spec is HBM else value
        for value, spec in zip(inputs, specs)
    ]
    return pl.pallas_call(
        kernel,
        out_shape=out,
        in_specs=specs,
        out_specs=jax.tree.map(lambda _: home, out),
        scratch_shapes=list(scratch),
        cost_estimate=pl.CostEstimate(flops=flops, bytes_accessed=moved, transcendentals=0),
        compiler_params=pltpu.CompilerParams(vmem_limit_bytes=16 << 20),
    )(*inputs)


def pieces(value, count=3):
    out = []
    for _ in range(count):
        out.append(value.astype(BF16))
        value = value - out[-1].astype(F32)
    return out


def split(value):
    return pieces(value, 2)


def mixed(tail, mix_ref, at):
    total = None
    for piece in range(mix_ref.shape[0]):
        part = lax.dot_general(
            tail, mix_ref[piece, :, at : at + tail.shape[1]], NT, preferred_element_type=F32
        )
        total = part if total is None else total + part
    return total


def join(ref, at, width):
    high = ref[:, at : at + width].astype(F32)
    return high + ref[:, at + width : at + 2 * width].astype(F32)


def fetch(sources, targets, sems):
    copies = [
        pltpu.make_async_copy(source, target, sems.at[index])
        for index, (source, target) in enumerate(zip(sources, targets))
    ]
    for copy in copies:
        copy.start()
    return copies


def first_kernel(grad_hbm, basis_hbm, out_ref, own_ref, grad_ref, basis_ref, sems):
    rank, rows = basis_ref.shape
    copies = fetch((grad_hbm, basis_hbm), (grad_ref, basis_ref), sems)
    copies[0].wait()
    rounded = grad_ref[...].astype(BF16)
    out_ref[:, :rows] = rounded
    own_ref[...] = rounded
    copies[1].wait()
    partial = lax.dot_general(rounded, basis_ref[...], NT, preferred_element_type=F32)
    high, low = split(partial)
    out_ref[:, rows : rows + rank] = high
    out_ref[:, rows + rank :] = low


def table_kernel(*refs):
    tiles_hbm, inputs, (mix_ref, flag_ref, tiles_ref) = refs[0], refs[1:6], refs[6:9]
    held, sems = refs[9:14], refs[14]
    count_ref, offset_ref, source_ref, far_ref, cores_ref = held
    owner = lax.axis_index("cell")
    slots, rank, _ = cores_ref.shape
    copies = fetch((*inputs, tiles_hbm.at[0]), (*held, tiles_ref), sems)
    for copy in copies[:-1]:
        copy.wait()
    cells = mix_ref.shape[2] // (2 * rank)
    used = far_ref[owner]
    for step in range(cells):
        total = jnp.zeros((rank, rank), F32)
        for slot in range(slots):
            hit = jnp.logical_and(source_ref[owner, slot] == (owner ^ step), slot < used)
            total = total + jnp.where(hit, cores_ref[slot], 0.0)
        for piece, value in enumerate(pieces(total)):
            for twin in range(2):
                at = (2 * step + twin) * rank
                mix_ref[piece, :, at : at + rank] = value
    beyond = owner ^ 2
    asked = beyond + offset_ref[beyond] == owner ^ 1
    beside = offset_ref[owner] + owner == owner ^ 1
    double = count_ref[owner] == 2
    for row, value in enumerate((asked, beside, double)):
        flag_ref[row] = jnp.full(flag_ref.shape[1:], value.astype(F32), F32)
    copies[-1].wait()


def pick(flag_ref, row, yes, no):
    shape = yes.shape
    mask = jnp.broadcast_to(flag_ref[row][:1, :1], shape) > 0.5
    return jnp.where(mask, yes.astype(F32), no.astype(F32)).astype(BF16)


def second_kernel(flag_ref, mine_ref, near_ref, out_ref, *, rows):
    out_ref[:, :rows] = pick(flag_ref, 0, near_ref[:, :rows], mine_ref[:, :rows])
    tail = mine_ref.shape[1] - rows
    out_ref[:, rows : rows + tail] = mine_ref[:, rows:]
    out_ref[:, rows + tail :] = near_ref[:, rows:]


def early_kernel(mix_ref, mine_ref, near_ref, after_ref, out_ref, *, rows):
    del after_ref
    tail = mine_ref.shape[1] - rows
    core = mixed(mine_ref[:, rows:], mix_ref, 0)
    out_ref[...] = core + mixed(near_ref[:, rows:], mix_ref, tail)


def third_kernel(flag_ref, mix_ref, core_ref, near_ref, far_ref, out_ref, *, rows):
    rank = core_ref.shape[1]
    beside = pick(flag_ref, 1, near_ref[:, :rows], far_ref[:, :rows])
    out_ref[:, :rows] = pick(flag_ref, 2, beside, jnp.zeros_like(beside))
    tail = near_ref.shape[1] - rows
    high, low = split(core_ref[...] + mixed(far_ref[:, rows:], mix_ref, 2 * tail))
    out_ref[:, rows : rows + rank] = high
    out_ref[:, rows + rank :] = low


def widen_kernel(mine_ref, other_ref, out_ref, *, rows):
    rank = (mine_ref.shape[1] - rows) // 2
    out_ref[:, :rows] = other_ref[:, :rows]
    high, low = split(join(mine_ref, rows, rank) + join(other_ref, rows, rank))
    out_ref[:, rows : rows + rank] = high
    out_ref[:, rows + rank :] = low


def stage_kernel(tiles_hbm, tiles_ref, sems):
    for copy in fetch((tiles_hbm.at[0],), (tiles_ref,), sems):
        copy.wait()


def numbered(order, step=0):
    return [(item, part, spot ^ step) for item, (part, spot) in enumerate(order)]


def near(total, held_ref, tiles, order):
    place = lax.axis_index("col")
    rows = tiles[0].shape[0]
    for item, part, spot in order:
        columns = pl.ds(pl.multiple_of((place ^ spot) * rows, rows), rows)
        total = total + lax.dot_general(
            held_ref[:, item * rows : (item + 1) * rows],
            tiles[part][:, columns],
            NT,
            preferred_element_type=F32,
        )
    return total


def early_near_kernel(
    held_ref, own_ref, tiles_hbm, basis_hbm, out_ref, tiles_ref, basis_ref, sems, *, order
):
    copies = fetch((tiles_hbm.at[1], basis_hbm), (tiles_ref, basis_ref), sems)
    tiles = (own_ref, tiles_ref)
    ready = [entry for entry in order if entry[1] == 0]
    total = near(jnp.zeros(out_ref.shape, F32), held_ref, tiles, ready)
    for copy in copies:
        copy.wait()
    out_ref[...] = near(total, held_ref, tiles, [entry for entry in order if entry[1] == 1])


def near_kernel(sum_ref, early_ref, late_ref, own_ref, tiles_ref, out_ref, *, early, late):
    tiles = (own_ref, tiles_ref)
    out_ref[...] = near(near(sum_ref[...], late_ref, tiles, late), early_ref, tiles, early)


def last_kernel(
    sum_ref, mine_ref, other_ref, basis_ref, own_ref, tiles_ref, out_ref, *, order
):
    rank, rows = basis_ref.shape
    core = (join(mine_ref, rows, rank) + join(other_ref, rows, rank)).astype(BF16)
    far = jnp.dot(core, basis_ref[...], preferred_element_type=F32)
    out_ref[...] = near(sum_ref[...] + far, other_ref, (own_ref, tiles_ref), order)


def swap(value, axis, step):
    size = lax.axis_size(axis)
    return lax.ppermute(value, axis, [(i, i ^ step) for i in range(size)])


def shifted(value, axis, by):
    size = lax.axis_size(axis)
    return lax.ppermute(value, axis, [(i, i + by) for i in range(size) if 0 <= i + by < size])


def over_small_chain(first, tables, cores, tiles):
    width, length = first.shape
    rows, rank = tiles.shape[1], cores.shape[1]
    beyond = swap(first, "cell", 1)
    mix, flags, own_tile = call(
        table_kernel,
        (
            jax.ShapeDtypeStruct((3, rank, 8 * rank), BF16),
            jax.ShapeDtypeStruct((3, 8, 128), F32),
            jax.ShapeDtypeStruct(tiles.shape[1:], tiles.dtype),
        ),
        (tiles, *tables, cores),
        [HBM] * 6,
        scratch=[
            *(pltpu.SMEM(table.shape, table.dtype) for table in tables),
            pltpu.VMEM(cores.shape, cores.dtype),
            pltpu.SemaphoreType.DMA((6,)),
        ],
        moved=cores.size * 4 + tiles.size,
    )
    second = call(
        functools.partial(second_kernel, rows=rows),
        jax.ShapeDtypeStruct((width, 2 * length - rows), BF16),
        (flags, first, beyond),
        [VMEM] * 3,
        moved=4 * first.size,
    )
    far = swap(second, "cell", 2)
    core = call(
        functools.partial(early_kernel, rows=rows),
        jax.ShapeDtypeStruct((width, rank), F32),
        (mix, first, beyond, second),
        [VMEM] * 4,
        moved=8 * first.size,
    )
    third = call(
        functools.partial(third_kernel, rows=rows),
        jax.ShapeDtypeStruct((width, length), BF16),
        (flags, mix, core, beyond, far),
        [VMEM] * 5,
        moved=8 * first.size,
    )
    return third, own_tile


def over_long_chain(first, tables, cores, tiles):
    owner = lax.axis_index("cell")
    rows, rank = tiles.shape[1], cores.shape[1]
    own_tile = call(
        stage_kernel,
        jax.ShapeDtypeStruct(tiles.shape[1:], tiles.dtype),
        (tiles,),
        [HBM],
        scratch=[pltpu.SemaphoreType.DMA((1,))],
        moved=tiles.size,
    )
    counts, offsets, sources, used = (table[owner] for table in tables)
    steps = [step for step in range(-REACH, REACH + 1) if step]
    moved = jnp.stack([shifted(first[:, :rows], "cell", -step) for step in steps])
    beside = lax.dynamic_index_in_dim(
        moved, offsets + REACH - (offsets > 0).astype(jnp.int32), 0, keepdims=False
    )
    beside = jnp.where(counts == 2, beside, jnp.zeros_like(beside))
    high, low = first[:, rows : rows + rank], first[:, rows + rank :]
    partial = high.astype(F32) + low.astype(F32)
    table = lax.all_gather(partial[None], "cell", axis=0, tiled=True)
    picked = jnp.take(table, sources, axis=0)
    slots = jnp.arange(cores.shape[0], dtype=jnp.int32)
    masked = jnp.where((slots < used)[:, None, None], cores, jnp.zeros_like(cores))
    core = jnp.einsum("kab,kwb->wa", masked, picked, precision=lax.Precision.HIGHEST)
    return jnp.concatenate((beside, *split(core)), axis=1), own_tile


def body(
    grad, near_tiles, tile_count, near_offset, far_src, far_count, far_cores, basis_out, basis_in
):
    rows, width = grad.shape
    rank = basis_in.shape[1]
    cells, parts = lax.axis_size("cell"), lax.axis_size("col")
    first, own = call(
        first_kernel,
        (
            jax.ShapeDtypeStruct((width, rows + 2 * rank), BF16),
            jax.ShapeDtypeStruct((width, rows), BF16),
        ),
        (grad.T, basis_in.T),
        [HBM] * 2,
        scratch=[
            pltpu.VMEM((width, rows), grad.dtype),
            pltpu.VMEM((rank, rows), basis_in.dtype),
            pltpu.SemaphoreType.DMA((2,)),
        ],
        moved=8 * grad.size,
    )
    tables = (tile_count, near_offset, far_src, far_count)
    tiles = near_tiles[0]
    over_cells = over_small_chain if cells == 2 * REACH else over_long_chain
    late, own_tile = over_cells(first, tables, far_cores[0], tiles)
    late_order = [(1, 0)]
    early, early_order = own, [(0, 0)]
    steps = [1 << bit for bit in reversed(range(parts.bit_length() - 1))]
    for step in steps:
        early_other = swap(early, "col", step)
        late_other = swap(late, "col", step)
        across = [(part, spot ^ step) for part, spot in early_order]
        if step > 1:
            early = jnp.concatenate((early, early_other, late[:, :rows]), axis=1)
            early_order = early_order + across + late_order
            late_order = [(part, spot ^ step) for part, spot in late_order]
            late = call(
                functools.partial(widen_kernel, rows=rows),
                jax.ShapeDtypeStruct(late.shape, BF16),
                (late, late_other),
                [VMEM] * 2,
                moved=8 * late.size,
            )
    total, other_tile, basis = call(
        functools.partial(early_near_kernel, order=numbered(early_order)),
        (
            jax.ShapeDtypeStruct((width, rows), F32),
            jax.ShapeDtypeStruct(tiles.shape[1:], tiles.dtype),
            jax.ShapeDtypeStruct((rank, rows), basis_out.dtype),
        ),
        (early, own_tile, tiles, basis_out.T),
        [VMEM, VMEM, HBM, HBM],
        scratch=[pltpu.SemaphoreType.DMA((2,))],
        flops=tiles.size * width,
        moved=tiles.size,
    )
    total = call(
        functools.partial(near_kernel, early=numbered(across), late=numbered(late_order)),
        jax.ShapeDtypeStruct((width, rows), F32),
        (total, early_other, late, own_tile, other_tile),
        [VMEM] * 5,
        flops=tiles.size * width,
        moved=tiles.size,
    )
    out = call(
        functools.partial(last_kernel, order=numbered(late_order, 1)),
        jax.ShapeDtypeStruct((width, rows), F32),
        (total, late, late_other, basis, own_tile, other_tile),
        [VMEM] * 6,
        flops=tiles.size * width,
        moved=tiles.size,
    )
    return out.T


def solution(mesh):
    placed = (
        P(("chain", "cell", "col"), None),
        P("cell", None, "col", None),
        P(),
        P(),
        P(),
        P(),
        P("cell", None, None, None),
        P(("cell", "col"), None),
        P(("cell", "col"), None),
    )

    return jax.shard_map(
        body,
        mesh=mesh,
        in_specs=placed,
        out_specs=P(("chain", "cell", "col"), None),
        check_vma=False,
    )
```

time: 21.7 us -> 23.1 us (1.065)
  starting transfers between devices: 7.78 us -> 9.32 us
    ppermute x4 -> x6, starting transfers between devices: 7.78 us -> 9.32 us  [swap(): return lax.ppermute(value, axis, [(i, i ^ step) for i in range(size)])]
    pallas_call x8 -> x9, Pallas kernels: 7.38 us -> 7.18 us  [call(): pl.pallas_call(kernel, out_shape=out, in_specs=specs, out_specs=jax.tree....]
    ppermute x4 -> x6, waiting for transfers between devices: 6.32 us -> 6.37 us  [swap(): return lax.ppermute(value, axis, [(i, i ^ step) for i in range(size)])]
  transfers between devices with their start and end apart: 4 -> 6, of which waited for: 4 -> 4; matrix products, arithmetic and copies ran while one was open for 0% -> 0% of each run, Pallas kernels for 19% -> 22%
where the time goes in v3:
time: 23.1 us; the launch traced here: 23 us
  starting transfers between devices  9.32 us (40%)
  Pallas kernels  7.18 us (31%)
  waiting for transfers between devices  6.37 us (28%)
    ppermute x6, starting transfers between devices, swap(): return lax.ppermute(value, axis, [(i, i ^ step) for i in range(size)])  9.32 us
    pallas_call x9, Pallas kernels, call(): pl.pallas_call(kernel, out_shape=out, in_specs=specs, out_specs=jax.tree....  7.18 us
    ppermute x6, waiting for transfers between devices, swap(): return lax.ppermute(value, axis, [(i, i ^ step) for i in range(size)])  6.37 us
  transfers between devices with their start and end apart: 6, of which 4 were waited for; matrix products, arithmetic and copies ran while one was open for 0% of the time, Pallas kernels for 22%

profile of v3, /device:TPU:0, one launch (start us, length us, event | category | flops | bytes accessed | tf_op | source)
XLA Modules:
  0.0 23.0 jit_solution(5559180187783992439)
XLA Ops:
  0.0 1.2 %shard_map.91 = (bf16[64,640]{1,0:T(8,128)(2,1)S(1)}, bf16[64,512]{1,0:T(8,128)(2,1)S(1)}) custom-call(f32[64,512]{1,0:T(8,128)} %bitcast.9, bf16[64,512]{1,0:T(8,128)(2,1)} %bitcast.11), custom_call_target="tpu_custom_call" | custom-call | bytes 262144 | tf_op jit(solution)/shard_map/pallas_call | solution.py:24
  1.2 3.1 %collective-permute-start.1 = (bf16[64,640]{1,0:T(8,128)(2,1)S(1)}, bf16[64,640]{1,0:T(8,128)(2,1)S(1)}, u32[]{:S(2)}, u32[]{:S(2)}) collective-permute-start(bf16[64,640]{1,0:T(8,128)(2,1)S(1)} %get-tuple-element.16.mine_ref), channel_id=1, source_target_pairs={{0,4},{4,0},{8,12},{12,8},{1,5},{5,1},{9,13},{13,9},{2,6},{6,2},{1... | collective-permute-start | bytes 245768 | tf_op jit(solution)/shard_map/ppermute | solution.py:204
  4.3 1.7 %shard_map.92 = (bf16[3,64,512]{2,1,0:T(8,128)(2,1)S(1)}, f32[3,8,128]{2,1,0:T(8,128)S(1)}, bf16[512,2048]{1,0:T(8,128)(2,1)S(1)}) custom-call(bf16[2,512,2048]{2,1,0:T(8,128)(2,1)} %bitcast.6, s32[4]{0:T(128)} %refs_1_.1, s32[4]{0:T(128)} %refs_2_.1, s32[4,8]{1,0:T(4,128)} %refs_3_.1, s32[4]{0:T(128)} %refs_4_.1, f32[8,64,64]{2,1,0:T(8,128)} %bitcast.8), custom_call_target="tpu_custom_call" | custom-call | bytes 2228224 | tf_op jit(solution)/shard_map/pallas_call | solution.py:24
  6.0 0.7 %collective-permute-done.1.near_ref = bf16[64,640]{1,0:T(8,128)(2,1)S(1)} collective-permute-done((bf16[64,640]{1,0:T(8,128)(2,1)S(1)}, bf16[64,640]{1,0:T(8,128)(2,1)S(1)}, u32[]{:S(2)}, u32[]{:S(2)}) %collective-permute-start.1) | collective-permute-done | bytes 81952 | tf_op jit(solution)/shard_map/ppermute | solution.py:204
  6.8 3.1 %collective-permute-start.2 = (bf16[64,768]{1,0:T(8,128)(2,1)S(1)}, bf16[64,768]{1,0:T(8,128)(2,1)S(1)}, u32[]{:S(2)}, u32[]{:S(2)}) collective-permute-start(bf16[64,768]{1,0:T(8,128)(2,1)S(1)} %shard_map.93.after_ref), channel_id=1, source_target_pairs={{0,8},{4,12},{8,0},{12,4},{1,9},{5,13},{9,1},{13,5},{2,10},{6,14},... | collective-permute-start | bytes 294920 | tf_op jit(solution)/shard_map/ppermute | solution.py:204
  9.9 1.5 %collective-permute-start = (bf16[64,512]{1,0:T(8,128)(2,1)S(1)}, bf16[64,512]{1,0:T(8,128)(2,1)S(1)}, u32[]{:S(2)}, u32[]{:S(2)}) collective-permute-start(bf16[64,512]{1,0:T(8,128)(2,1)S(1)} %get-tuple-element.13), channel_id=1, source_target_pairs={{0,2},{1,3},{2,0},{3,1},{4,6},{5,7},{6,4},{7,5},{8,10},{9,11},{10,... | collective-permute-start | bytes 196616 | tf_op jit(solution)/shard_map/ppermute | solution.py:204
  11.3 0.1 shard_map.94.core_ref
  11.5 1.3 %collective-permute-done.2.far_ref = bf16[64,768]{1,0:T(8,128)(2,1)S(1)} collective-permute-done((bf16[64,768]{1,0:T(8,128)(2,1)S(1)}, bf16[64,768]{1,0:T(8,128)(2,1)S(1)}, u32[]{:S(2)}, u32[]{:S(2)}) %collective-permute-start.2) | collective-permute-done | bytes 98336 | tf_op jit(solution)/shard_map/ppermute | solution.py:204
  12.8 0.2 %shard_map.95.mine_ref = bf16[64,640]{1,0:T(8,128)(2,1)S(1)} custom-call(f32[3,8,128]{2,1,0:T(8,128)S(1)} %get-tuple-element.14.flag_ref, bf16[3,64,512]{2,1,0:T(8,128)(2,1)S(1)} %get-tuple-element.15.mix_ref, f32[64,64]{1,0:T(8,128)S(1)} %shard_map.94.core_ref, bf16[64,640]{1,0:T(8,128)(2,1)S(1)} %collective-permute-done.1.near_ref, ...), custom_call_target="tpu_custom_call" | custom-call | bytes 327680 | tf_op jit(solution)/shard_map/pallas_call | solution.py:24
  13.0 1.1 %collective-permute-done = bf16[64,512]{1,0:T(8,128)(2,1)S(1)} collective-permute-done((bf16[64,512]{1,0:T(8,128)(2,1)S(1)}, bf16[64,512]{1,0:T(8,128)(2,1)S(1)}, u32[]{:S(2)}, u32[]{:S(2)}) %collective-permute-start) | collective-permute-done | bytes 65568 | tf_op jit(solution)/shard_map/ppermute | solution.py:204
  14.1 0.1 collective-permute-start.3
  14.2 1.6 %collective-permute-start.4 = (bf16[64,640]{1,0:T(8,128)(2,1)S(1)}, bf16[64,640]{1,0:T(8,128)(2,1)S(1)}, u32[]{:S(2)}, u32[]{:S(2)}) collective-permute-start(bf16[64,640]{1,0:T(8,128)(2,1)S(1)} %shard_map.95.mine_ref), channel_id=1, source_target_pairs={{0,2},{1,3},{2,0},{3,1},{4,6},{5,7},{6,4},{7,5},{8,10},{9,11},{10,... | collective-permute-start | bytes 245768 | tf_op jit(solution)/shard_map/ppermute | solution.py:204
  15.8 3.3 %collective-permute-done.4.other_ref = bf16[64,640]{1,0:T(8,128)(2,1)S(1)} collective-permute-done((bf16[64,640]{1,0:T(8,128)(2,1)S(1)}, bf16[64,640]{1,0:T(8,128)(2,1)S(1)}, u32[]{:S(2)}, u32[]{:S(2)}) %collective-permute-start.4) | collective-permute-done | bytes 81952 | tf_op jit(solution)/shard_map/ppermute | solution.py:204
  19.1 0.2 shard_map.97.late_ref.mine_ref
  19.2 0.0 collective-permute-start.5
  19.2 1.9 %shard_map.96 = (f32[64,512]{1,0:T(8,128)S(1)}, bf16[512,2048]{1,0:T(8,128)(2,1)S(1)}, bf16[64,512]{1,0:T(8,128)(2,1)S(1)}) custom-call(bf16[64,1536]{1,0:T(8,128)(2,1)S(1)} %pad_maximum_fusion.held_ref, bf16[512,2048]{1,0:T(8,128)(2,1)S(1)} %get-tuple-element.17.own_ref, bf16[2,512,2048]{2,1,0:T(8,128)(2,1)} %bitcast.7, bf16[64,512]{1,0:T(8,128)(2,1)} %bitcast.10), custom_call_target="tpu_custom_call" | custom-call | flops 134217728 | bytes 2097152 | tf_op jit(solution)/shard_map/pallas_call | solution.py:24
  21.2 0.0 collective-permute-done.3.early_ref
  21.2 0.8 %shard_map.98.sum_ref = f32[64,512]{1,0:T(8,128)S(1)} custom-call(f32[64,512]{1,0:T(8,128)S(1)} %get-tuple-element.18.sum_ref, bf16[64,1536]{1,0:T(8,128)(2,1)S(1)} %collective-permute-done.3.early_ref, bf16[64,640]{1,0:T(8,128)(2,1)S(1)} %shard_map.97.late_ref.mine_ref, bf16[512,2048]{1,0:T(8,128)(2,1)S(1)} %get-tuple-element.17.own_ref, ...), custom_call_target="tpu_custom_call" | custom-call | flops 134217728 | bytes 2097152 | tf_op jit(solution)/shard_map/pallas_call | solution.py:24
  21.9 0.0 collective-permute-done.5.other_ref
  21.9 1.0 %shard_map.99 = f32[64,512]{1,0:T(8,128)} custom-call(f32[64,512]{1,0:T(8,128)S(1)} %shard_map.98.sum_ref, bf16[64,640]{1,0:T(8,128)(2,1)S(1)} %shard_map.97.late_ref.mine_ref, bf16[64,640]{1,0:T(8,128)(2,1)S(1)} %collective-permute-done.5.other_ref, bf16[64,512]{1,0:T(8,128)(2,1)S(1)} %get-tuple-element.20.basis_ref, ...), custom_call_target="tpu_custom_call" | custom-call | flops 134217728 | bytes 2097152 | tf_op jit(solution)/shard_map/pallas_call | solution.py:24
  (3 shorter events, 0.1 us)
Async XLA Ops:
  1.2 5.6 %collective-permute-start.1 = (bf16[64,640]{1,0:T(8,128)(2,1)S(1)}, bf16[64,640]{1,0:T(8,128)(2,1)S(1)}, u32[]{:S(2)}, u32[]{:S(2)}) collective-permute-start(bf16[64,640]{1,0:T(8,128)(2,1)S(1)} %get-tuple-element.16.mine_ref), channel_id=1, source_target_pairs={{0,4},{4,0},{8,12},{12,8},{1,5},{5,1},{9,13},{13,9},{2,6},{6,2},{1... | collective-permute-start | bytes 245768 | tf_op jit(solution)/shard_map/ppermute | solution.py:204
  6.8 6.0 %collective-permute-start.2 = (bf16[64,768]{1,0:T(8,128)(2,1)S(1)}, bf16[64,768]{1,0:T(8,128)(2,1)S(1)}, u32[]{:S(2)}, u32[]{:S(2)}) collective-permute-start(bf16[64,768]{1,0:T(8,128)(2,1)S(1)} %shard_map.93.after_ref), channel_id=1, source_target_pairs={{0,8},{4,12},{8,0},{12,4},{1,9},{5,13},{9,1},{13,5},{2,10},{6,14},... | collective-permute-start | bytes 294920 | tf_op jit(solution)/shard_map/ppermute | solution.py:204
  9.9 4.3 %collective-permute-start = (bf16[64,512]{1,0:T(8,128)(2,1)S(1)}, bf16[64,512]{1,0:T(8,128)(2,1)S(1)}, u32[]{:S(2)}, u32[]{:S(2)}) collective-permute-start(bf16[64,512]{1,0:T(8,128)(2,1)S(1)} %get-tuple-element.13), channel_id=1, source_target_pairs={{0,2},{1,3},{2,0},{3,1},{4,6},{5,7},{6,4},{7,5},{8,10},{9,11},{10,... | collective-permute-start | bytes 196616 | tf_op jit(solution)/shard_map/ppermute | solution.py:204
  14.1 7.0 %collective-permute-start.3 = (bf16[64,1536]{1,0:T(8,128)(2,1)S(1)}, bf16[64,1536]{1,0:T(8,128)(2,1)S(1)}, u32[]{:S(2)}, u32[]{:S(2)}) collective-permute-start(bf16[64,1536]{1,0:T(8,128)(2,1)S(1)} %pad_maximum_fusion.held_ref), channel_id=1, source_target_pairs={{0,1},{1,0},{2,3},{3,2},{4,5},{5,4},{6,7},{7,6},{8,9},{9,8},{10,11... | collective-permute-start | bytes 589832 | tf_op jit(solution)/shard_map/ppermute | solution.py:204
  14.2 4.8 %collective-permute-start.4 = (bf16[64,640]{1,0:T(8,128)(2,1)S(1)}, bf16[64,640]{1,0:T(8,128)(2,1)S(1)}, u32[]{:S(2)}, u32[]{:S(2)}) collective-permute-start(bf16[64,640]{1,0:T(8,128)(2,1)S(1)} %shard_map.95.mine_ref), channel_id=1, source_target_pairs={{0,2},{1,3},{2,0},{3,1},{4,6},{5,7},{6,4},{7,5},{8,10},{9,11},{10,... | collective-permute-start | bytes 245768 | tf_op jit(solution)/shard_map/ppermute | solution.py:204
  19.2 2.7 %collective-permute-start.5 = (bf16[64,640]{1,0:T(8,128)(2,1)S(1)}, bf16[64,640]{1,0:T(8,128)(2,1)S(1)}, u32[]{:S(2)}, u32[]{:S(2)}) collective-permute-start(bf16[64,640]{1,0:T(8,128)(2,1)S(1)} %shard_map.97.late_ref.mine_ref), channel_id=1, source_target_pairs={{0,1},{1,0},{2,3},{3,2},{4,5},{5,4},{6,7},{7,6},{8,9},{9,8},{10,11... | collective-permute-start | bytes 245768 | tf_op jit(solution)/shard_map/ppermute | solution.py:204

commit v4 on v3

--- a/solution.py
+++ b/solution.py
@@ -94,28 +94,33 @@
         copy.wait()
     cells = mix_ref.shape[2] // (2 * rank)
     used = far_ref[owner]
+    place = lax.axis_index("col")
+    steps = [cell_step(place, stage) for stage in range(2)]
     for step in range(cells):
         total = jnp.zeros((rank, rank), F32)
+        source = owner ^ (steps[0] * (step & 1)) ^ (steps[1] * (step >> 1))
         for slot in range(slots):
-            hit = jnp.logical_and(source_ref[owner, slot] == (owner ^ step), slot < used)
+            hit = jnp.logical_and(source_ref[owner, slot] == source, slot < used)
             total = total + jnp.where(hit, cores_ref[slot], 0.0)
         for piece, value in enumerate(pieces(total)):
             for twin in range(2):
                 at = (2 * step + twin) * rank
                 mix_ref[piece, :, at : at + rank] = value
-    beyond = owner ^ 2
-    asked = beyond + offset_ref[beyond] == owner ^ 1
-    beside = offset_ref[owner] + owner == owner ^ 1
+    beyond = owner ^ steps[1]
+    asked = beyond + offset_ref[beyond] == owner ^ steps[0]
+    beside = offset_ref[owner] + owner == owner ^ steps[0]
     double = count_ref[owner] == 2
     for row, value in enumerate((asked, beside, double)):
         flag_ref[row] = jnp.full(flag_ref.shape[1:], value.astype(F32), F32)
     copies[-1].wait()
 
 
-def pick(flag_ref, row, yes, no):
-    shape = yes.shape
-    mask = jnp.broadcast_to(flag_ref[row][:1, :1], shape) > 0.5
-    return jnp.where(mask, yes.astype(F32), no.astype(F32)).astype(BF16)
+def pick(flag_ref, row, yes, no, use=None):
+    mask = jnp.broadcast_to(flag_ref[row][:1, :1], yes.shape) > 0.5
+    value = jnp.where(mask, yes.astype(F32), no.astype(F32))
+    if use is not None:
+        value = jnp.where(use > 0.5, value, 0.0)
+    return value.astype(BF16)
 
 
 def second_kernel(flag_ref, mine_ref, near_ref, out_ref, *, rows):
@@ -134,38 +139,30 @@
 
 def third_kernel(flag_ref, mix_ref, core_ref, near_ref, far_ref, out_ref, *, rows):
     rank = core_ref.shape[1]
-    beside = pick(flag_ref, 1, near_ref[:, :rows], far_ref[:, :rows])
-    out_ref[:, :rows] = pick(flag_ref, 2, beside, jnp.zeros_like(beside))
+    use = jnp.broadcast_to(flag_ref[2][:1, :1], (far_ref.shape[0], rows))
+    out_ref[:, :rows] = pick(flag_ref, 1, near_ref[:, :rows], far_ref[:, :rows], use)
     tail = near_ref.shape[1] - rows
     high, low = split(core_ref[...] + mixed(far_ref[:, rows:], mix_ref, 2 * tail))
     out_ref[:, rows : rows + rank] = high
     out_ref[:, rows + rank :] = low
 
 
-def widen_kernel(mine_ref, other_ref, out_ref, *, rows):
-    rank = (mine_ref.shape[1] - rows) // 2
-    out_ref[:, :rows] = other_ref[:, :rows]
-    high, low = split(join(mine_ref, rows, rank) + join(other_ref, rows, rank))
-    out_ref[:, rows : rows + rank] = high
-    out_ref[:, rows + rank :] = low
-
-
 def stage_kernel(tiles_hbm, tiles_ref, sems):
     for copy in fetch((tiles_hbm.at[0],), (tiles_ref,), sems):
         copy.wait()
 
 
-def numbered(order, step=0):
-    return [(item, part, spot ^ step) for item, (part, spot) in enumerate(order)]
+def flipped(items, step, at=0):
+    return [(lane + at, part, spot ^ step) for lane, part, spot in items]
 
 
 def near(total, held_ref, tiles, order):
     place = lax.axis_index("col")
     rows = tiles[0].shape[0]
-    for item, part, spot in order:
+    for lane, part, spot in order:
         columns = pl.ds(pl.multiple_of((place ^ spot) * rows, rows), rows)
         total = total + lax.dot_general(
-            held_ref[:, item * rows : (item + 1) * rows],
+            held_ref[:, lane : lane + rows],
             tiles[part][:, columns],
             NT,
             preferred_element_type=F32,
@@ -185,18 +182,24 @@
     out_ref[...] = near(total, held_ref, tiles, [entry for entry in order if entry[1] == 1])
 
 
-def near_kernel(sum_ref, early_ref, late_ref, own_ref, tiles_ref, out_ref, *, early, late):
+def near_kernel(
+    sum_ref, mine_ref, early_ref, late_ref, own_ref, tiles_ref, out_ref, core_ref, *, early, late, cores
+):
     tiles = (own_ref, tiles_ref)
     out_ref[...] = near(near(sum_ref[...], late_ref, tiles, late), early_ref, tiles, early)
+    core = jnp.zeros(core_ref.shape, F32)
+    for ref, lanes in zip((mine_ref, early_ref, late_ref), cores):
+        for lane in lanes:
+            core = core + join(ref, lane, core.shape[1])
+    core_ref[...] = core
 
 
 def last_kernel(
-    sum_ref, mine_ref, other_ref, basis_ref, own_ref, tiles_ref, out_ref, *, order
+    sum_ref, core_ref, other_ref, basis_ref, own_ref, tiles_ref, out_ref, *, late, lane
 ):
-    rank, rows = basis_ref.shape
-    core = (join(mine_ref, rows, rank) + join(other_ref, rows, rank)).astype(BF16)
+    core = (core_ref[...] + join(other_ref, lane, core_ref.shape[1])).astype(BF16)
     far = jnp.dot(core, basis_ref[...], preferred_element_type=F32)
-    out_ref[...] = near(sum_ref[...] + far, other_ref, (own_ref, tiles_ref), order)
+    out_ref[...] = near(sum_ref[...] + far, other_ref, (own_ref, tiles_ref), late)
 
 
 def swap(value, axis, step):
@@ -204,6 +207,20 @@
     return lax.ppermute(value, axis, [(i, i ^ step) for i in range(size)])
 
 
+def cell_step(place, stage):
+    return 1 + (place + stage + 1) % 2
+
+
+def crossed(value, stage):
+    cells, parts = lax.axis_size("cell"), lax.axis_size("col")
+    pairs = [
+        (cell * parts + place, (cell ^ cell_step(place, stage)) * parts + place)
+        for cell in range(cells)
+        for place in range(parts)
+    ]
+    return lax.ppermute(value, ("cell", "col"), pairs)
+
+
 def shifted(value, axis, by):
     size = lax.axis_size(axis)
     return lax.ppermute(value, axis, [(i, i + by) for i in range(size) if 0 <= i + by < size])
@@ -212,7 +229,7 @@
 def over_small_chain(first, tables, cores, tiles):
     width, length = first.shape
     rows, rank = tiles.shape[1], cores.shape[1]
-    beyond = swap(first, "cell", 1)
+    beyond = crossed(first, 0)
     mix, flags, own_tile = call(
         table_kernel,
         (
@@ -236,7 +253,7 @@
         [VMEM] * 3,
         moved=4 * first.size,
     )
-    far = swap(second, "cell", 2)
+    far = crossed(second, 1)
     core = call(
         functools.partial(early_kernel, rows=rows),
         jax.ShapeDtypeStruct((width, rank), F32),
@@ -307,26 +324,20 @@
     tiles = near_tiles[0]
     over_cells = over_small_chain if cells == 2 * REACH else over_long_chain
     late, own_tile = over_cells(first, tables, far_cores[0], tiles)
-    late_order = [(1, 0)]
-    early, early_order = own, [(0, 0)]
+    late_items, early_items = [(0, 1, 0)], [(0, 0, 0)]
+    early, early_cores = own, []
     steps = [1 << bit for bit in reversed(range(parts.bit_length() - 1))]
     for step in steps:
         early_other = swap(early, "col", step)
         late_other = swap(late, "col", step)
-        across = [(part, spot ^ step) for part, spot in early_order]
         if step > 1:
-            early = jnp.concatenate((early, early_other, late[:, :rows]), axis=1)
-            early_order = early_order + across + late_order
-            late_order = [(part, spot ^ step) for part, spot in late_order]
-            late = call(
-                functools.partial(widen_kernel, rows=rows),
-                jax.ShapeDtypeStruct(late.shape, BF16),
-                (late, late_other),
-                [VMEM] * 2,
-                moved=8 * late.size,
-            )
+            size = early.shape[1]
+            early = jnp.concatenate((early, early_other, late), axis=1)
+            early_items += flipped(early_items, step, size) + flipped(late_items, 0, 2 * size)
+            early_cores += [lane + size for lane in early_cores] + [2 * size + rows]
+            late, late_items = late_other, flipped(late_items, step)
     total, other_tile, basis = call(
-        functools.partial(early_near_kernel, order=numbered(early_order)),
+        functools.partial(early_near_kernel, order=early_items),
         (
             jax.ShapeDtypeStruct((width, rows), F32),
             jax.ShapeDtypeStruct(tiles.shape[1:], tiles.dtype),
@@ -338,18 +349,26 @@
         flops=tiles.size * width,
         moved=tiles.size,
     )
-    total = call(
-        functools.partial(near_kernel, early=numbered(across), late=numbered(late_order)),
-        jax.ShapeDtypeStruct((width, rows), F32),
-        (total, early_other, late, own_tile, other_tile),
-        [VMEM] * 5,
+    total, core = call(
+        functools.partial(
+            near_kernel,
+            early=flipped(early_items, 1),
+            late=late_items,
+            cores=(early_cores, early_cores, [rows]),
+        ),
+        (
+            jax.ShapeDtypeStruct((width, rows), F32),
+            jax.ShapeDtypeStruct((width, rank), F32),
+        ),
+        (total, early, early_other, late, own_tile, other_tile),
+        [VMEM] * 6,
         flops=tiles.size * width,
         moved=tiles.size,
     )
     out = call(
-        functools.partial(last_kernel, order=numbered(late_order, 1)),
+        functools.partial(last_kernel, late=flipped(late_items, 1), lane=rows),
         jax.ShapeDtypeStruct((width, rows), F32),
-        (total, late, late_other, basis, own_tile, other_tile),
+        (total, core, late_other, basis, own_tile, other_tile),
         [VMEM] * 6,
         flops=tiles.size * width,
         moved=tiles.size,

time: 23.1 us -> 22.9 us (level)
    ppermute x6 -> x4, starting transfers between devices: 9.32 us -> 3.12 us  [swap(): return lax.ppermute(value, axis, [(i, i ^ step) for i in range(size)])]
    ppermute x0 -> x2, starting transfers between devices: none -> 6.1 us  [crossed(): return lax.ppermute(value, ('cell', 'col'), pairs)]
    ppermute x6 -> x4, waiting for transfers between devices: 6.37 us -> 4.61 us  [swap(): return lax.ppermute(value, axis, [(i, i ^ step) for i in range(size)])]
    ppermute x0 -> x2, waiting for transfers between devices: none -> 1.74 us  [crossed(): return lax.ppermute(value, ('cell', 'col'), pairs)]
    pallas_call x9 -> x8, Pallas kernels: 7.18 us -> 7.03 us  [call(): pl.pallas_call(kernel, out_shape=out, in_specs=specs, out_specs=jax.tree....]
  transfers between devices with their start and end apart: 6 -> 6, of which waited for: 4 -> 4; matrix products, arithmetic and copies ran while one was open for 0% -> 0% of each run, Pallas kernels for 22% -> 21%
where the time goes in v4:
time: 22.9 us; the launch traced here: 22.7 us
  starting transfers between devices  9.22 us (40%)
  Pallas kernels  7.03 us (31%)
  waiting for transfers between devices  6.35 us (28%)
    pallas_call x8, Pallas kernels, call(): pl.pallas_call(kernel, out_shape=out, in_specs=specs, out_specs=jax.tree....  7.03 us
    ppermute x2, starting transfers between devices, crossed(): return lax.ppermute(value, ('cell', 'col'), pairs)  6.1 us
    ppermute x4, waiting for transfers between devices, swap(): return lax.ppermute(value, axis, [(i, i ^ step) for i in range(size)])  4.61 us
    ppermute x4, starting transfers between devices, swap(): return lax.ppermute(value, axis, [(i, i ^ step) for i in range(size)])  3.12 us
    ppermute x2, waiting for transfers between devices, crossed(): return lax.ppermute(value, ('cell', 'col'), pairs)  1.74 us
  transfers between devices with their start and end apart: 6, of which 4 were waited for; matrix products, arithmetic and copies ran while one was open for 0% of the time, Pallas kernels for 21%

profile of v4, /device:TPU:0, one launch (start us, length us, event | category | flops | bytes accessed | tf_op | source)
XLA Modules:
  0.0 22.7 jit_solution(6008423357771605131)
XLA Ops:
  0.0 1.2 %shard_map.91 = (bf16[64,640]{1,0:T(8,128)(2,1)S(1)}, bf16[64,512]{1,0:T(8,128)(2,1)S(1)}) custom-call(f32[64,512]{1,0:T(8,128)} %bitcast.9, bf16[64,512]{1,0:T(8,128)(2,1)} %bitcast.11), custom_call_target="tpu_custom_call" | custom-call | bytes 262144 | tf_op jit(solution)/shard_map/pallas_call | solution.py:24
  1.2 4.1 %collective-permute-start.1 = (bf16[64,640]{1,0:T(8,128)(2,1)S(1)}, bf16[64,640]{1,0:T(8,128)(2,1)S(1)}, u32[]{:S(2)}, u32[]{:S(2)}) collective-permute-start(bf16[64,640]{1,0:T(8,128)(2,1)S(1)} %get-tuple-element.18.mine_ref), channel_id=1, source_target_pairs={{0,8},{1,5},{2,10},{3,7},{4,12},{5,1},{6,14},{7,3},{8,0},{9,13},{1... | collective-permute-start | bytes 245768 | tf_op jit(solution)/shard_map/ppermute | solution.py:221
  5.3 1.7 %shard_map.92 = (bf16[3,64,512]{2,1,0:T(8,128)(2,1)S(1)}, f32[3,8,128]{2,1,0:T(8,128)S(1)}, bf16[512,2048]{1,0:T(8,128)(2,1)S(1)}) custom-call(bf16[2,512,2048]{2,1,0:T(8,128)(2,1)} %bitcast.6, s32[4]{0:T(128)} %refs_1_.1, s32[4]{0:T(128)} %refs_2_.1, s32[4,8]{1,0:T(4,128)} %refs_3_.1, s32[4]{0:T(128)} %refs_4_.1, f32[8,64,64]{2,1,0:T(8,128)} %bitcast.8), custom_call_target="tpu_custom_call" | custom-call | bytes 2228224 | tf_op jit(solution)/shard_map/pallas_call | solution.py:24
  7.0 0.7 %collective-permute-done.1.near_ref = bf16[64,640]{1,0:T(8,128)(2,1)S(1)} collective-permute-done((bf16[64,640]{1,0:T(8,128)(2,1)S(1)}, bf16[64,640]{1,0:T(8,128)(2,1)S(1)}, u32[]{:S(2)}, u32[]{:S(2)}) %collective-permute-start.1) | collective-permute-done | bytes 81952 | tf_op jit(solution)/shard_map/ppermute | solution.py:221
  7.8 2.0 %collective-permute-start.2 = (bf16[64,768]{1,0:T(8,128)(2,1)S(1)}, bf16[64,768]{1,0:T(8,128)(2,1)S(1)}, u32[]{:S(2)}, u32[]{:S(2)}) collective-permute-start(bf16[64,768]{1,0:T(8,128)(2,1)S(1)} %shard_map.93.after_ref), channel_id=1, source_target_pairs={{0,4},{1,9},{2,6},{3,11},{4,0},{5,13},{6,2},{7,15},{8,12},{9,1},{1... | collective-permute-start | bytes 294920 | tf_op jit(solution)/shard_map/ppermute | solution.py:221
  9.7 1.5 %collective-permute-start = (bf16[64,512]{1,0:T(8,128)(2,1)S(1)}, bf16[64,512]{1,0:T(8,128)(2,1)S(1)}, u32[]{:S(2)}, u32[]{:S(2)}) collective-permute-start(bf16[64,512]{1,0:T(8,128)(2,1)S(1)} %get-tuple-element.15), channel_id=1, source_target_pairs={{0,2},{1,3},{2,0},{3,1},{4,6},{5,7},{6,4},{7,5},{8,10},{9,11},{10,... | collective-permute-start | bytes 196616 | tf_op jit(solution)/shard_map/ppermute | solution.py:207
  11.2 0.1 shard_map.94.core_ref
  11.4 1.1 %collective-permute-done.2.far_ref = bf16[64,768]{1,0:T(8,128)(2,1)S(1)} collective-permute-done((bf16[64,768]{1,0:T(8,128)(2,1)S(1)}, bf16[64,768]{1,0:T(8,128)(2,1)S(1)}, u32[]{:S(2)}, u32[]{:S(2)}) %collective-permute-start.2) | collective-permute-done | bytes 98336 | tf_op jit(solution)/shard_map/ppermute | solution.py:221
  12.5 0.2 %shard_map.95 = bf16[64,640]{1,0:T(8,128)(2,1)S(1)} custom-call(f32[3,8,128]{2,1,0:T(8,128)S(1)} %get-tuple-element.16.flag_ref, bf16[3,64,512]{2,1,0:T(8,128)(2,1)S(1)} %get-tuple-element.17.mix_ref, f32[64,64]{1,0:T(8,128)S(1)} %shard_map.94.core_ref, bf16[64,640]{1,0:T(8,128)(2,1)S(1)} %collective-permute-done.1.near_ref, ...), custom_call_target="tpu_custom_call" | custom-call | bytes 327680 | tf_op jit(solution)/shard_map/pallas_call | solution.py:24
  12.7 1.3 %collective-permute-done = bf16[64,512]{1,0:T(8,128)(2,1)S(1)} collective-permute-done((bf16[64,512]{1,0:T(8,128)(2,1)S(1)}, bf16[64,512]{1,0:T(8,128)(2,1)S(1)}, u32[]{:S(2)}, u32[]{:S(2)}) %collective-permute-start) | collective-permute-done | bytes 65568 | tf_op jit(solution)/shard_map/ppermute | solution.py:207
  14.0 0.1 collective-permute-start.3
  14.1 1.6 %collective-permute-start.4 = (bf16[64,640]{1,0:T(8,128)(2,1)S(1)}, bf16[64,640]{1,0:T(8,128)(2,1)S(1)}, u32[]{:S(2)}, u32[]{:S(2)}) collective-permute-start(bf16[64,640]{1,0:T(8,128)(2,1)S(1)} %shard_map.95), channel_id=1, source_target_pairs={{0,2},{1,3},{2,0},{3,1},{4,6},{5,7},{6,4},{7,5},{8,10},{9,11},{10,... | collective-permute-start | bytes 245768 | tf_op jit(solution)/shard_map/ppermute | solution.py:207
  15.7 3.3 %collective-permute-done.4.late_ref = bf16[64,640]{1,0:T(8,128)(2,1)S(1)} collective-permute-done((bf16[64,640]{1,0:T(8,128)(2,1)S(1)}, bf16[64,640]{1,0:T(8,128)(2,1)S(1)}, u32[]{:S(2)}, u32[]{:S(2)}) %collective-permute-start.4) | collective-permute-done | bytes 81952 | tf_op jit(solution)/shard_map/ppermute | solution.py:207
  19.0 0.0 collective-permute-start.5
  19.0 1.9 %shard_map.96 = (f32[64,512]{1,0:T(8,128)S(1)}, bf16[512,2048]{1,0:T(8,128)(2,1)S(1)}, bf16[64,512]{1,0:T(8,128)(2,1)S(1)}) custom-call(bf16[64,1664]{1,0:T(8,128)(2,1)S(1)} %pad_maximum_fusion.held_ref.mine_ref, bf16[512,2048]{1,0:T(8,128)(2,1)S(1)} %get-tuple-element.19.own_ref, bf16[2,512,2048]{2,1,0:T(8,128)(2,1)} %bitcast.7, bf16[64,512]{1,0:T(8,128)(2,1)} %bitcast.10), custom_call_target="tpu_custom_call" | custom-call | flops 134217728 | bytes 2097152 | tf_op jit(solution)/shard_map/pallas_call | solution.py:24
  20.9 0.0 collective-permute-done.3.early_ref
  20.9 0.8 %shard_map.97 = (f32[64,512]{1,0:T(8,128)S(1)}, f32[64,64]{1,0:T(8,128)S(1)}) custom-call(f32[64,512]{1,0:T(8,128)S(1)} %get-tuple-element.20.sum_ref, bf16[64,1664]{1,0:T(8,128)(2,1)S(1)} %pad_maximum_fusion.held_ref.mine_ref, bf16[64,1664]{1,0:T(8,128)(2,1)S(1)} %collective-permute-done.3.early_ref, bf16[64,640]{1,0:T(8,128)(2,1)S(1)} %collective-permute-done.4.late_ref, ...), custom_call_target="tpu_custom_call" | custom-call | flops 134217728 | bytes 2097152 | tf_op jit(solution)/shard_map/pallas_call | solution.py:24
  21.6 0.0 collective-permute-done.5.other_ref
  21.7 1.0 %shard_map.98 = f32[64,512]{1,0:T(8,128)} custom-call(f32[64,512]{1,0:T(8,128)S(1)} %get-tuple-element.22.sum_ref, f32[64,64]{1,0:T(8,128)S(1)} %get-tuple-element.23.core_ref, bf16[64,640]{1,0:T(8,128)(2,1)S(1)} %collective-permute-done.5.other_ref, bf16[64,512]{1,0:T(8,128)(2,1)S(1)} %get-tuple-element.24.basis_ref, ...), custom_call_target="tpu_custom_call" | custom-call | flops 134217728 | bytes 2097152 | tf_op jit(solution)/shard_map/pallas_call | solution.py:24
  (2 shorter events, 0.1 us)
Async XLA Ops:
  1.2 6.6 %collective-permute-start.1 = (bf16[64,640]{1,0:T(8,128)(2,1)S(1)}, bf16[64,640]{1,0:T(8,128)(2,1)S(1)}, u32[]{:S(2)}, u32[]{:S(2)}) collective-permute-start(bf16[64,640]{1,0:T(8,128)(2,1)S(1)} %get-tuple-element.18.mine_ref), channel_id=1, source_target_pairs={{0,8},{1,5},{2,10},{3,7},{4,12},{5,1},{6,14},{7,3},{8,0},{9,13},{1... | collective-permute-start | bytes 245768 | tf_op jit(solution)/shard_map/ppermute | solution.py:221
  7.8 4.7 %collective-permute-start.2 = (bf16[64,768]{1,0:T(8,128)(2,1)S(1)}, bf16[64,768]{1,0:T(8,128)(2,1)S(1)}, u32[]{:S(2)}, u32[]{:S(2)}) collective-permute-start(bf16[64,768]{1,0:T(8,128)(2,1)S(1)} %shard_map.93.after_ref), channel_id=1, source_target_pairs={{0,4},{1,9},{2,6},{3,11},{4,0},{5,13},{6,2},{7,15},{8,12},{9,1},{1... | collective-permute-start | bytes 294920 | tf_op jit(solution)/shard_map/ppermute | solution.py:221
  9.7 4.3 %collective-permute-start = (bf16[64,512]{1,0:T(8,128)(2,1)S(1)}, bf16[64,512]{1,0:T(8,128)(2,1)S(1)}, u32[]{:S(2)}, u32[]{:S(2)}) collective-permute-start(bf16[64,512]{1,0:T(8,128)(2,1)S(1)} %get-tuple-element.15), channel_id=1, source_target_pairs={{0,2},{1,3},{2,0},{3,1},{4,6},{5,7},{6,4},{7,5},{8,10},{9,11},{10,... | collective-permute-start | bytes 196616 | tf_op jit(solution)/shard_map/ppermute | solution.py:207
  14.0 6.8 %collective-permute-start.3 = (bf16[64,1664]{1,0:T(8,128)(2,1)S(1)}, bf16[64,1664]{1,0:T(8,128)(2,1)S(1)}, u32[]{:S(2)}, u32[]{:S(2)}) collective-permute-start(bf16[64,1664]{1,0:T(8,128)(2,1)S(1)} %pad_maximum_fusion.held_ref.mine_ref), channel_id=1, source_target_pairs={{0,1},{1,0},{2,3},{3,2},{4,5},{5,4},{6,7},{7,6},{8,9},{9,8},{10,11... | collective-permute-start | bytes 638984 | tf_op jit(solution)/shard_map/ppermute | solution.py:207
  14.1 4.8 %collective-permute-start.4 = (bf16[64,640]{1,0:T(8,128)(2,1)S(1)}, bf16[64,640]{1,0:T(8,128)(2,1)S(1)}, u32[]{:S(2)}, u32[]{:S(2)}) collective-permute-start(bf16[64,640]{1,0:T(8,128)(2,1)S(1)} %shard_map.95), channel_id=1, source_target_pairs={{0,2},{1,3},{2,0},{3,1},{4,6},{5,7},{6,4},{7,5},{8,10},{9,11},{10,... | collective-permute-start | bytes 245768 | tf_op jit(solution)/shard_map/ppermute | solution.py:207
  19.0 2.7 %collective-permute-start.5 = (bf16[64,640]{1,0:T(8,128)(2,1)S(1)}, bf16[64,640]{1,0:T(8,128)(2,1)S(1)}, u32[]{:S(2)}, u32[]{:S(2)}) collective-permute-start(bf16[64,640]{1,0:T(8,128)(2,1)S(1)} %collective-permute-done.4.late_ref), channel_id=1, source_target_pairs={{0,1},{1,0},{2,3},{3,2},{4,5},{5,4},{6,7},{7,6},{8,9},{9,8},{10,11... | collective-permute-start | bytes 245768 | tf_op jit(solution)/shard_map/ppermute | solution.py:207

commit v5 on v4

--- a/solution.py
+++ b/solution.py
@@ -9,6 +9,8 @@
 
 
 REACH = 2
+PIECES = 3
+CUTS = 2
 F32 = jnp.float32
 BF16 = jnp.bfloat16
 VMEM = pl.BlockSpec(memory_space=pltpu.VMEM)
@@ -32,7 +34,7 @@
     )(*inputs)
 
 
-def pieces(value, count=3):
+def pieces(value, count):
     out = []
     for _ in range(count):
         out.append(value.astype(BF16))
@@ -40,18 +42,16 @@
     return out
 
 
-def split(value):
-    return pieces(value, 2)
-
-
-def mixed(tail, mix_ref, at):
-    total = None
-    for piece in range(mix_ref.shape[0]):
-        part = lax.dot_general(
-            tail, mix_ref[piece, :, at : at + tail.shape[1]], NT, preferred_element_type=F32
-        )
-        total = part if total is None else total + part
-    return total
+def twins(value):
+    rank = value.shape[1] // 2
+    high = value.astype(BF16).astype(F32)
+    lane = lax.broadcasted_iota(jnp.int32, value.shape, 1)
+    return jnp.where(lane < rank, high, value - high).astype(BF16)
+
+
+def mixed(tails, mix_ref, group):
+    held = jnp.concatenate(tails * PIECES, axis=1)
+    return jnp.dot(held, mix_ref[group], preferred_element_type=F32)
 
 
 def join(ref, at, width):
@@ -69,18 +69,25 @@
     return copies
 
 
+def cut(ref):
+    lines = ref.shape[0] // CUTS
+    return [ref.at[pl.ds(index * lines, lines)] for index in range(CUTS)]
+
+
 def first_kernel(grad_hbm, basis_hbm, out_ref, own_ref, grad_ref, basis_ref, sems):
-    rank, rows = basis_ref.shape
-    copies = fetch((grad_hbm, basis_hbm), (grad_ref, basis_ref), sems)
-    copies[0].wait()
+    rows = basis_ref.shape[1]
+    copies = fetch(
+        [*cut(basis_hbm), *cut(grad_hbm)], [*cut(basis_ref), *cut(grad_ref)], sems
+    )
+    for copy in copies:
+        copy.wait()
     rounded = grad_ref[...].astype(BF16)
     out_ref[:, :rows] = rounded
     own_ref[...] = rounded
-    copies[1].wait()
-    partial = lax.dot_general(rounded, basis_ref[...], NT, preferred_element_type=F32)
-    high, low = split(partial)
-    out_ref[:, rows : rows + rank] = high
-    out_ref[:, rows + rank :] = low
+    basis = basis_ref[...]
+    doubled = jnp.concatenate((basis, basis), axis=0)
+    partial = lax.dot_general(rounded, doubled, NT, preferred_element_type=F32)
+    out_ref[:, rows:] = twins(partial)
 
 
 def table_kernel(*refs):
@@ -92,20 +99,20 @@
     copies = fetch((*inputs, tiles_hbm.at[0]), (*held, tiles_ref), sems)
     for copy in copies[:-1]:
         copy.wait()
-    cells = mix_ref.shape[2] // (2 * rank)
     used = far_ref[owner]
     place = lax.axis_index("col")
     steps = [cell_step(place, stage) for stage in range(2)]
-    for step in range(cells):
+    for step in range(4):
         total = jnp.zeros((rank, rank), F32)
         source = owner ^ (steps[0] * (step & 1)) ^ (steps[1] * (step >> 1))
         for slot in range(slots):
             hit = jnp.logical_and(source_ref[owner, slot] == source, slot < used)
             total = total + jnp.where(hit, cores_ref[slot], 0.0)
-        for piece, value in enumerate(pieces(total)):
+        total = total.T
+        for piece, value in enumerate(pieces(jnp.concatenate((total, total), axis=1), PIECES)):
             for twin in range(2):
-                at = (2 * step + twin) * rank
-                mix_ref[piece, :, at : at + rank] = value
+                at = (4 * piece + 2 * (step % 2) + twin) * rank
+                mix_ref[step // 2, at : at + rank, :] = value
     beyond = owner ^ steps[1]
     asked = beyond + offset_ref[beyond] == owner ^ steps[0]
     beside = offset_ref[owner] + owner == owner ^ steps[0]
@@ -132,19 +139,13 @@
 
 def early_kernel(mix_ref, mine_ref, near_ref, after_ref, out_ref, *, rows):
     del after_ref
-    tail = mine_ref.shape[1] - rows
-    core = mixed(mine_ref[:, rows:], mix_ref, 0)
-    out_ref[...] = core + mixed(near_ref[:, rows:], mix_ref, tail)
+    out_ref[...] = mixed([mine_ref[:, rows:], near_ref[:, rows:]], mix_ref, 0)
 
 
 def third_kernel(flag_ref, mix_ref, core_ref, near_ref, far_ref, out_ref, *, rows):
-    rank = core_ref.shape[1]
     use = jnp.broadcast_to(flag_ref[2][:1, :1], (far_ref.shape[0], rows))
     out_ref[:, :rows] = pick(flag_ref, 1, near_ref[:, :rows], far_ref[:, :rows], use)
-    tail = near_ref.shape[1] - rows
-    high, low = split(core_ref[...] + mixed(far_ref[:, rows:], mix_ref, 2 * tail))
-    out_ref[:, rows : rows + rank] = high
-    out_ref[:, rows + rank :] = low
+    out_ref[:, rows:] = twins(core_ref[...] + mixed([far_ref[:, rows:]], mix_ref, 1))
 
 
 def stage_kernel(tiles_hbm, tiles_ref, sems):
@@ -233,7 +234,7 @@
     mix, flags, own_tile = call(
         table_kernel,
         (
-            jax.ShapeDtypeStruct((3, rank, 8 * rank), BF16),
+            jax.ShapeDtypeStruct((2, 4 * PIECES * rank, 2 * rank), BF16),
             jax.ShapeDtypeStruct((3, 8, 128), F32),
             jax.ShapeDtypeStruct(tiles.shape[1:], tiles.dtype),
         ),
@@ -256,7 +257,7 @@
     far = crossed(second, 1)
     core = call(
         functools.partial(early_kernel, rows=rows),
-        jax.ShapeDtypeStruct((width, rank), F32),
+        jax.ShapeDtypeStruct((width, 2 * rank), F32),
         (mix, first, beyond, second),
         [VMEM] * 4,
         moved=8 * first.size,
@@ -296,7 +297,7 @@
     slots = jnp.arange(cores.shape[0], dtype=jnp.int32)
     masked = jnp.where((slots < used)[:, None, None], cores, jnp.zeros_like(cores))
     core = jnp.einsum("kab,kwb->wa", masked, picked, precision=lax.Precision.HIGHEST)
-    return jnp.concatenate((beside, *split(core)), axis=1), own_tile
+    return jnp.concatenate((beside, *pieces(core, 2)), axis=1), own_tile
 
 
 def body(
@@ -316,7 +317,7 @@
         scratch=[
             pltpu.VMEM((width, rows), grad.dtype),
             pltpu.VMEM((rank, rows), basis_in.dtype),
-            pltpu.SemaphoreType.DMA((2,)),
+            pltpu.SemaphoreType.DMA((2 * CUTS,)),
         ],
         moved=8 * grad.size,
     )

time: 22.9 us -> 22.9 us (level)
  no operation moved by 1% of the time
where the time goes in v5:
time: 22.9 us; the launch traced here: 22.6 us
  starting transfers between devices  9.22 us (40%)
  Pallas kernels  6.93 us (30%)
  waiting for transfers between devices  6.39 us (28%)
    pallas_call x8, Pallas kernels, call(): pl.pallas_call(kernel, out_shape=out, in_specs=specs, out_specs=jax.tree....  6.93 us
    ppermute x2, starting transfers between devices, crossed(): return lax.ppermute(value, ('cell', 'col'), pairs)  6.1 us
    ppermute x4, waiting for transfers between devices, swap(): return lax.ppermute(value, axis, [(i, i ^ step) for i in range(size)])  4.67 us
    ppermute x4, starting transfers between devices, swap(): return lax.ppermute(value, axis, [(i, i ^ step) for i in range(size)])  3.12 us
    ppermute x2, waiting for transfers between devices, crossed(): return lax.ppermute(value, ('cell', 'col'), pairs)  1.72 us
  transfers between devices with their start and end apart: 6, of which 4 were waited for; matrix products, arithmetic and copies ran while one was open for 0% of the time, Pallas kernels for 21%

profile of v5, /device:TPU:0, one launch (start us, length us, event | category | flops | bytes accessed | tf_op | source)
XLA Modules:
  0.0 22.6 jit_solution(16870670362795856329)
XLA Ops:
  0.0 1.1 %shard_map.91 = (bf16[64,640]{1,0:T(8,128)(2,1)S(1)}, bf16[64,512]{1,0:T(8,128)(2,1)S(1)}) custom-call(f32[64,512]{1,0:T(8,128)} %bitcast.9, bf16[64,512]{1,0:T(8,128)(2,1)} %bitcast.11), custom_call_target="tpu_custom_call" | custom-call | bytes 262144 | tf_op jit(solution)/shard_map/pallas_call | solution.py:26
  1.1 4.1 %collective-permute-start.1 = (bf16[64,640]{1,0:T(8,128)(2,1)S(1)}, bf16[64,640]{1,0:T(8,128)(2,1)S(1)}, u32[]{:S(2)}, u32[]{:S(2)}) collective-permute-start(bf16[64,640]{1,0:T(8,128)(2,1)S(1)} %get-tuple-element.18.mine_ref), channel_id=1, source_target_pairs={{0,8},{1,5},{2,10},{3,7},{4,12},{5,1},{6,14},{7,3},{8,0},{9,13},{1... | collective-permute-start | bytes 245768 | tf_op jit(solution)/shard_map/ppermute | solution.py:222
  5.3 1.7 %shard_map.92 = (bf16[2,768,128]{2,1,0:T(8,128)(2,1)S(1)}, f32[3,8,128]{2,1,0:T(8,128)S(1)}, bf16[512,2048]{1,0:T(8,128)(2,1)S(1)}) custom-call(bf16[2,512,2048]{2,1,0:T(8,128)(2,1)} %bitcast.6, s32[4]{0:T(128)} %refs_1_.1, s32[4]{0:T(128)} %refs_2_.1, s32[4,8]{1,0:T(4,128)} %refs_3_.1, s32[4]{0:T(128)} %refs_4_.1, f32[8,64,64]{2,1,0:T(8,128)} %bitcast.8), custom_call_target="tpu_custom_call" | custom-call | bytes 2228224 | tf_op jit(solution)/shard_map/pallas_call | solution.py:26
  7.0 0.7 %collective-permute-done.1.near_ref = bf16[64,640]{1,0:T(8,128)(2,1)S(1)} collective-permute-done((bf16[64,640]{1,0:T(8,128)(2,1)S(1)}, bf16[64,640]{1,0:T(8,128)(2,1)S(1)}, u32[]{:S(2)}, u32[]{:S(2)}) %collective-permute-start.1) | collective-permute-done | bytes 81952 | tf_op jit(solution)/shard_map/ppermute | solution.py:222
  7.7 2.0 %collective-permute-start.2 = (bf16[64,768]{1,0:T(8,128)(2,1)S(1)}, bf16[64,768]{1,0:T(8,128)(2,1)S(1)}, u32[]{:S(2)}, u32[]{:S(2)}) collective-permute-start(bf16[64,768]{1,0:T(8,128)(2,1)S(1)} %shard_map.93.after_ref), channel_id=1, source_target_pairs={{0,4},{1,9},{2,6},{3,11},{4,0},{5,13},{6,2},{7,15},{8,12},{9,1},{1... | collective-permute-start | bytes 294920 | tf_op jit(solution)/shard_map/ppermute | solution.py:222
  9.7 1.5 %collective-permute-start = (bf16[64,512]{1,0:T(8,128)(2,1)S(1)}, bf16[64,512]{1,0:T(8,128)(2,1)S(1)}, u32[]{:S(2)}, u32[]{:S(2)}) collective-permute-start(bf16[64,512]{1,0:T(8,128)(2,1)S(1)} %get-tuple-element.15), channel_id=1, source_target_pairs={{0,2},{1,3},{2,0},{3,1},{4,6},{5,7},{6,4},{7,5},{8,10},{9,11},{10,... | collective-permute-start | bytes 196616 | tf_op jit(solution)/shard_map/ppermute | solution.py:208
  11.2 0.2 shard_map.94.core_ref
  11.4 1.0 %collective-permute-done.2.far_ref = bf16[64,768]{1,0:T(8,128)(2,1)S(1)} collective-permute-done((bf16[64,768]{1,0:T(8,128)(2,1)S(1)}, bf16[64,768]{1,0:T(8,128)(2,1)S(1)}, u32[]{:S(2)}, u32[]{:S(2)}) %collective-permute-start.2) | collective-permute-done | bytes 98336 | tf_op jit(solution)/shard_map/ppermute | solution.py:222
  12.4 0.2 shard_map.95
  12.6 1.4 %collective-permute-done = bf16[64,512]{1,0:T(8,128)(2,1)S(1)} collective-permute-done((bf16[64,512]{1,0:T(8,128)(2,1)S(1)}, bf16[64,512]{1,0:T(8,128)(2,1)S(1)}, u32[]{:S(2)}, u32[]{:S(2)}) %collective-permute-start) | collective-permute-done | bytes 65568 | tf_op jit(solution)/shard_map/ppermute | solution.py:208
  14.0 0.1 collective-permute-start.3
  14.1 1.6 %collective-permute-start.4 = (bf16[64,640]{1,0:T(8,128)(2,1)S(1)}, bf16[64,640]{1,0:T(8,128)(2,1)S(1)}, u32[]{:S(2)}, u32[]{:S(2)}) collective-permute-start(bf16[64,640]{1,0:T(8,128)(2,1)S(1)} %shard_map.95), channel_id=1, source_target_pairs={{0,2},{1,3},{2,0},{3,1},{4,6},{5,7},{6,4},{7,5},{8,10},{9,11},{10,... | collective-permute-start | bytes 245768 | tf_op jit(solution)/shard_map/ppermute | solution.py:208
  15.6 3.3 %collective-permute-done.4.late_ref = bf16[64,640]{1,0:T(8,128)(2,1)S(1)} collective-permute-done((bf16[64,640]{1,0:T(8,128)(2,1)S(1)}, bf16[64,640]{1,0:T(8,128)(2,1)S(1)}, u32[]{:S(2)}, u32[]{:S(2)}) %collective-permute-start.4) | collective-permute-done | bytes 81952 | tf_op jit(solution)/shard_map/ppermute | solution.py:208
  18.9 0.0 collective-permute-start.5
  18.9 1.9 %shard_map.96 = (f32[64,512]{1,0:T(8,128)S(1)}, bf16[512,2048]{1,0:T(8,128)(2,1)S(1)}, bf16[64,512]{1,0:T(8,128)(2,1)S(1)}) custom-call(bf16[64,1664]{1,0:T(8,128)(2,1)S(1)} %pad_maximum_fusion.held_ref.mine_ref, bf16[512,2048]{1,0:T(8,128)(2,1)S(1)} %get-tuple-element.19.own_ref, bf16[2,512,2048]{2,1,0:T(8,128)(2,1)} %bitcast.7, bf16[64,512]{1,0:T(8,128)(2,1)} %bitcast.10), custom_call_target="tpu_custom_call" | custom-call | flops 134217728 | bytes 2097152 | tf_op jit(solution)/shard_map/pallas_call | solution.py:26
  20.8 0.0 collective-permute-done.3.early_ref
  20.8 0.8 %shard_map.97 = (f32[64,512]{1,0:T(8,128)S(1)}, f32[64,64]{1,0:T(8,128)S(1)}) custom-call(f32[64,512]{1,0:T(8,128)S(1)} %get-tuple-element.20.sum_ref, bf16[64,1664]{1,0:T(8,128)(2,1)S(1)} %pad_maximum_fusion.held_ref.mine_ref, bf16[64,1664]{1,0:T(8,128)(2,1)S(1)} %collective-permute-done.3.early_ref, bf16[64,640]{1,0:T(8,128)(2,1)S(1)} %collective-permute-done.4.late_ref, ...), custom_call_target="tpu_custom_call" | custom-call | flops 134217728 | bytes 2097152 | tf_op jit(solution)/shard_map/pallas_call | solution.py:26
  21.6 0.0 collective-permute-done.5.other_ref
  21.6 1.0 %shard_map.98 = f32[64,512]{1,0:T(8,128)} custom-call(f32[64,512]{1,0:T(8,128)S(1)} %get-tuple-element.22.sum_ref, f32[64,64]{1,0:T(8,128)S(1)} %get-tuple-element.23.core_ref, bf16[64,640]{1,0:T(8,128)(2,1)S(1)} %collective-permute-done.5.other_ref, bf16[64,512]{1,0:T(8,128)(2,1)S(1)} %get-tuple-element.24.basis_ref, ...), custom_call_target="tpu_custom_call" | custom-call | flops 134217728 | bytes 2097152 | tf_op jit(solution)/shard_map/pallas_call | solution.py:26
  (2 shorter events, 0.1 us)
Async XLA Ops:
  1.1 6.6 %collective-permute-start.1 = (bf16[64,640]{1,0:T(8,128)(2,1)S(1)}, bf16[64,640]{1,0:T(8,128)(2,1)S(1)}, u32[]{:S(2)}, u32[]{:S(2)}) collective-permute-start(bf16[64,640]{1,0:T(8,128)(2,1)S(1)} %get-tuple-element.18.mine_ref), channel_id=1, source_target_pairs={{0,8},{1,5},{2,10},{3,7},{4,12},{5,1},{6,14},{7,3},{8,0},{9,13},{1... | collective-permute-start | bytes 245768 | tf_op jit(solution)/shard_map/ppermute | solution.py:222
  7.7 4.7 %collective-permute-start.2 = (bf16[64,768]{1,0:T(8,128)(2,1)S(1)}, bf16[64,768]{1,0:T(8,128)(2,1)S(1)}, u32[]{:S(2)}, u32[]{:S(2)}) collective-permute-start(bf16[64,768]{1,0:T(8,128)(2,1)S(1)} %shard_map.93.after_ref), channel_id=1, source_target_pairs={{0,4},{1,9},{2,6},{3,11},{4,0},{5,13},{6,2},{7,15},{8,12},{9,1},{1... | collective-permute-start | bytes 294920 | tf_op jit(solution)/shard_map/ppermute | solution.py:222
  9.7 4.3 %collective-permute-start = (bf16[64,512]{1,0:T(8,128)(2,1)S(1)}, bf16[64,512]{1,0:T(8,128)(2,1)S(1)}, u32[]{:S(2)}, u32[]{:S(2)}) collective-permute-start(bf16[64,512]{1,0:T(8,128)(2,1)S(1)} %get-tuple-element.15), channel_id=1, source_target_pairs={{0,2},{1,3},{2,0},{3,1},{4,6},{5,7},{6,4},{7,5},{8,10},{9,11},{10,... | collective-permute-start | bytes 196616 | tf_op jit(solution)/shard_map/ppermute | solution.py:208
  14.0 6.8 %collective-permute-start.3 = (bf16[64,1664]{1,0:T(8,128)(2,1)S(1)}, bf16[64,1664]{1,0:T(8,128)(2,1)S(1)}, u32[]{:S(2)}, u32[]{:S(2)}) collective-permute-start(bf16[64,1664]{1,0:T(8,128)(2,1)S(1)} %pad_maximum_fusion.held_ref.mine_ref), channel_id=1, source_target_pairs={{0,1},{1,0},{2,3},{3,2},{4,5},{5,4},{6,7},{7,6},{8,9},{9,8},{10,11... | collective-permute-start | bytes 638984 | tf_op jit(solution)/shard_map/ppermute | solution.py:208
  14.1 4.8 %collective-permute-start.4 = (bf16[64,640]{1,0:T(8,128)(2,1)S(1)}, bf16[64,640]{1,0:T(8,128)(2,1)S(1)}, u32[]{:S(2)}, u32[]{:S(2)}) collective-permute-start(bf16[64,640]{1,0:T(8,128)(2,1)S(1)} %shard_map.95), channel_id=1, source_target_pairs={{0,2},{1,3},{2,0},{3,1},{4,6},{5,7},{6,4},{7,5},{8,10},{9,11},{10,... | collective-permute-start | bytes 245768 | tf_op jit(solution)/shard_map/ppermute | solution.py:208
  18.9 2.7 %collective-permute-start.5 = (bf16[64,640]{1,0:T(8,128)(2,1)S(1)}, bf16[64,640]{1,0:T(8,128)(2,1)S(1)}, u32[]{:S(2)}, u32[]{:S(2)}) collective-permute-start(bf16[64,640]{1,0:T(8,128)(2,1)S(1)} %collective-permute-done.4.late_ref), channel_id=1, source_target_pairs={{0,1},{1,0},{2,3},{3,2},{4,5},{5,4},{6,7},{7,6},{8,9},{9,8},{10,11... | collective-permute-start | bytes 245768 | tf_op jit(solution)/shard_map/ppermute | solution.py:208

commit v6 on v5

--- a/solution.py
+++ b/solution.py
@@ -10,6 +10,7 @@
 
 REACH = 2
 PIECES = 3
+AHEAD = 2
 CUTS = 2
 F32 = jnp.float32
 BF16 = jnp.bfloat16
@@ -18,7 +19,7 @@
 NT = (((1,), (1,)), ((), ()))
 
 
-def call(kernel, out, inputs, specs, home=VMEM, scratch=(), flops=0, moved=0):
+def call(kernel, out, inputs, specs, home=VMEM, scratch=(), flops=0, moved=0, alias=None):
     inputs = [
         pltpu.with_memory_space_constraint(value, pltpu.HBM) if spec is HBM else value
         for value, spec in zip(inputs, specs)
@@ -29,6 +30,7 @@
         in_specs=specs,
         out_specs=jax.tree.map(lambda _: home, out),
         scratch_shapes=list(scratch),
+        input_output_aliases=alias or {},
         cost_estimate=pl.CostEstimate(flops=flops, bytes_accessed=moved, transcendentals=0),
         compiler_params=pltpu.CompilerParams(vmem_limit_bytes=16 << 20),
     )(*inputs)
@@ -137,9 +139,24 @@
     out_ref[:, rows + tail :] = near_ref[:, rows:]
 
 
-def early_kernel(mix_ref, mine_ref, near_ref, after_ref, out_ref, *, rows):
+def leads():
+    return lax.axis_index("col") % 2 == 1
+
+
+def early_kernel(
+    mix_ref, mine_ref, near_ref, after_ref, tiles_hbm, out_ref, tiles_ref, sems, *, rows
+):
     del after_ref
+
+    @pl.when(leads())
+    def _():
+        pltpu.make_async_copy(tiles_hbm.at[1], tiles_ref, sems.at[0]).start()
+
     out_ref[...] = mixed([mine_ref[:, rows:], near_ref[:, rows:]], mix_ref, 0)
+
+    @pl.when(leads())
+    def _():
+        pltpu.make_async_copy(tiles_hbm.at[1], tiles_ref, sems.at[0]).wait()
 
 
 def third_kernel(flag_ref, mix_ref, core_ref, near_ref, far_ref, out_ref, *, rows):
@@ -148,8 +165,8 @@
     out_ref[:, rows:] = twins(core_ref[...] + mixed([far_ref[:, rows:]], mix_ref, 1))
 
 
-def stage_kernel(tiles_hbm, tiles_ref, sems):
-    for copy in fetch((tiles_hbm.at[0],), (tiles_ref,), sems):
+def stage_kernel(tiles_hbm, own_ref, other_ref, sems):
+    for copy in fetch((tiles_hbm.at[0], tiles_hbm.at[1]), (own_ref, other_ref), sems):
         copy.wait()
 
 
@@ -172,22 +189,48 @@
 
 
 def early_near_kernel(
-    held_ref, own_ref, tiles_hbm, basis_hbm, out_ref, tiles_ref, basis_ref, sems, *, order
+    held_ref, own_ref, held_tiles_ref, tiles_hbm, basis_hbm, out_ref, tiles_ref, basis_ref, sems, *, order
 ):
-    copies = fetch((tiles_hbm.at[1], basis_hbm), (tiles_ref, basis_ref), sems)
+    del held_tiles_ref
+    follows = jnp.logical_not(leads())
+
+    @pl.when(follows)
+    def _():
+        pltpu.make_async_copy(tiles_hbm.at[1], tiles_ref, sems.at[0]).start()
+
+    basis_copy = pltpu.make_async_copy(basis_hbm, basis_ref, sems.at[1])
+    basis_copy.start()
     tiles = (own_ref, tiles_ref)
     ready = [entry for entry in order if entry[1] == 0]
     total = near(jnp.zeros(out_ref.shape, F32), held_ref, tiles, ready)
-    for copy in copies:
-        copy.wait()
+
+    @pl.when(follows)
+    def _():
+        pltpu.make_async_copy(tiles_hbm.at[1], tiles_ref, sems.at[0]).wait()
+
     out_ref[...] = near(total, held_ref, tiles, [entry for entry in order if entry[1] == 1])
+    basis_copy.wait()
+
+
+def middle_kernel(sum_ref, early_ref, own_ref, tiles_ref, out_ref, *, order):
+    out_ref[...] = sum_ref[...]
+
+    @pl.when(leads())
+    def _():
+        out_ref[...] = near(sum_ref[...], early_ref, (own_ref, tiles_ref), order)
 
 
 def near_kernel(
     sum_ref, mine_ref, early_ref, late_ref, own_ref, tiles_ref, out_ref, core_ref, *, early, late, cores
 ):
     tiles = (own_ref, tiles_ref)
-    out_ref[...] = near(near(sum_ref[...], late_ref, tiles, late), early_ref, tiles, early)
+    total = near(sum_ref[...], late_ref, tiles, late)
+    out_ref[...] = near(total, early_ref, tiles, early[AHEAD:])
+
+    @pl.when(jnp.logical_not(leads()))
+    def _():
+        out_ref[...] = near(out_ref[...], early_ref, tiles, early[:AHEAD])
+
     core = jnp.zeros(core_ref.shape, F32)
     for ref, lanes in zip((mine_ref, early_ref, late_ref), cores):
         for lane in lanes:
@@ -198,9 +241,9 @@
 def last_kernel(
     sum_ref, core_ref, other_ref, basis_ref, own_ref, tiles_ref, out_ref, *, late, lane
 ):
+    total = near(sum_ref[...], other_ref, (own_ref, tiles_ref), late)
     core = (core_ref[...] + join(other_ref, lane, core_ref.shape[1])).astype(BF16)
-    far = jnp.dot(core, basis_ref[...], preferred_element_type=F32)
-    out_ref[...] = near(sum_ref[...] + far, other_ref, (own_ref, tiles_ref), late)
+    out_ref[...] = total + jnp.dot(core, basis_ref[...], preferred_element_type=F32)
 
 
 def swap(value, axis, step):
@@ -255,11 +298,15 @@
         moved=4 * first.size,
     )
     far = crossed(second, 1)
-    core = call(
+    core, other_tile = call(
         functools.partial(early_kernel, rows=rows),
-        jax.ShapeDtypeStruct((width, 2 * rank), F32),
-        (mix, first, beyond, second),
-        [VMEM] * 4,
+        (
+            jax.ShapeDtypeStruct((width, 2 * rank), F32),
+            jax.ShapeDtypeStruct(tiles.shape[1:], tiles.dtype),
+        ),
+        (mix, first, beyond, second, tiles),
+        [VMEM] * 4 + [HBM],
+        scratch=[pltpu.SemaphoreType.DMA((1,))],
         moved=8 * first.size,
     )
     third = call(
@@ -269,18 +316,18 @@
         [VMEM] * 5,
         moved=8 * first.size,
     )
-    return third, own_tile
+    return third, own_tile, other_tile
 
 
 def over_long_chain(first, tables, cores, tiles):
     owner = lax.axis_index("cell")
     rows, rank = tiles.shape[1], cores.shape[1]
-    own_tile = call(
+    own_tile, other_tile = call(
         stage_kernel,
-        jax.ShapeDtypeStruct(tiles.shape[1:], tiles.dtype),
+        (jax.ShapeDtypeStruct(tiles.shape[1:], tiles.dtype),) * 2,
         (tiles,),
         [HBM],
-        scratch=[pltpu.SemaphoreType.DMA((1,))],
+        scratch=[pltpu.SemaphoreType.DMA((2,))],
         moved=tiles.size,
     )
     counts, offsets, sources, used = (table[owner] for table in tables)
@@ -297,7 +344,7 @@
     slots = jnp.arange(cores.shape[0], dtype=jnp.int32)
     masked = jnp.where((slots < used)[:, None, None], cores, jnp.zeros_like(cores))
     core = jnp.einsum("kab,kwb->wa", masked, picked, precision=lax.Precision.HIGHEST)
-    return jnp.concatenate((beside, *pieces(core, 2)), axis=1), own_tile
+    return jnp.concatenate((beside, *pieces(core, 2)), axis=1), own_tile, other_tile
 
 
 def body(
@@ -324,7 +371,7 @@
     tables = (tile_count, near_offset, far_src, far_count)
     tiles = near_tiles[0]
     over_cells = over_small_chain if cells == 2 * REACH else over_long_chain
-    late, own_tile = over_cells(first, tables, far_cores[0], tiles)
+    late, own_tile, other_tile = over_cells(first, tables, far_cores[0], tiles)
     late_items, early_items = [(0, 1, 0)], [(0, 0, 0)]
     early, early_cores = own, []
     steps = [1 << bit for bit in reversed(range(parts.bit_length() - 1))]
@@ -344,16 +391,26 @@
             jax.ShapeDtypeStruct(tiles.shape[1:], tiles.dtype),
             jax.ShapeDtypeStruct((rank, rows), basis_out.dtype),
         ),
-        (early, own_tile, tiles, basis_out.T),
-        [VMEM, VMEM, HBM, HBM],
+        (early, own_tile, other_tile, tiles, basis_out.T),
+        [VMEM, VMEM, VMEM, HBM, HBM],
+        alias={2: 1},
         scratch=[pltpu.SemaphoreType.DMA((2,))],
         flops=tiles.size * width,
         moved=tiles.size,
     )
+    across = flipped(early_items, 1)
+    total = call(
+        functools.partial(middle_kernel, order=across[:AHEAD]),
+        jax.ShapeDtypeStruct((width, rows), F32),
+        (total, early_other, own_tile, other_tile),
+        [VMEM] * 4,
+        flops=tiles.size * width,
+        moved=tiles.size,
+    )
     total, core = call(
         functools.partial(
             near_kernel,
-            early=flipped(early_items, 1),
+            early=across,
             late=late_items,
             cores=(early_cores, early_cores, [rows]),
         ),

time: 22.9 us -> 23 us (level)
    pallas_call x8 -> x9, Pallas kernels: 6.93 us -> 7.12 us  [call(): pl.pallas_call(kernel, out_shape=out, in_specs=specs, out_specs=jax.tree....]
  transfers between devices with their start and end apart: 6 -> 6, of which waited for: 4 -> 4; matrix products, arithmetic and copies ran while one was open for 0% -> 0% of each run, Pallas kernels for 21% -> 22%
where the time goes in v6:
time: 23 us; the launch traced here: 22.8 us
  starting transfers between devices  9.22 us (40%)
  Pallas kernels  7.12 us (31%)
  waiting for transfers between devices  6.38 us (28%)
    pallas_call x9, Pallas kernels, call(): pl.pallas_call(kernel, out_shape=out, in_specs=specs, out_specs=jax.tree....  7.12 us
    ppermute x2, starting transfers between devices, crossed(): return lax.ppermute(value, ('cell', 'col'), pairs)  6.1 us
    ppermute x4, waiting for transfers between devices, swap(): return lax.ppermute(value, axis, [(i, i ^ step) for i in range(size)])  4.67 us
    ppermute x4, starting transfers between devices, swap(): return lax.ppermute(value, axis, [(i, i ^ step) for i in range(size)])  3.12 us
    ppermute x2, waiting for transfers between devices, crossed(): return lax.ppermute(value, ('cell', 'col'), pairs)  1.7 us
  transfers between devices with their start and end apart: 6, of which 4 were waited for; matrix products, arithmetic and copies ran while one was open for 0% of the time, Pallas kernels for 22%

profile of v6, /device:TPU:0, one launch (start us, length us, event | category | flops | bytes accessed | tf_op | source)
XLA Modules:
  0.0 22.8 jit_solution(6349055482536902065)
XLA Ops:
  0.0 1.1 %shard_map.91 = (bf16[64,640]{1,0:T(8,128)(2,1)S(1)}, bf16[64,512]{1,0:T(8,128)(2,1)S(1)}) custom-call(f32[64,512]{1,0:T(8,128)} %bitcast.10, bf16[64,512]{1,0:T(8,128)(2,1)} %bitcast.12), custom_call_target="tpu_custom_call" | custom-call | bytes 262144 | tf_op jit(solution)/shard_map/pallas_call | solution.py:27
  1.1 4.1 %collective-permute-start.1 = (bf16[64,640]{1,0:T(8,128)(2,1)S(1)}, bf16[64,640]{1,0:T(8,128)(2,1)S(1)}, u32[]{:S(2)}, u32[]{:S(2)}) collective-permute-start(bf16[64,640]{1,0:T(8,128)(2,1)S(1)} %get-tuple-element.20.mine_ref), channel_id=1, source_target_pairs={{0,8},{1,5},{2,10},{3,7},{4,12},{5,1},{6,14},{7,3},{8,0},{9,13},{1... | collective-permute-start | bytes 245768 | tf_op jit(solution)/shard_map/ppermute | solution.py:265
  5.3 1.7 %shard_map.92 = (bf16[2,768,128]{2,1,0:T(8,128)(2,1)S(1)}, f32[3,8,128]{2,1,0:T(8,128)S(1)}, bf16[512,2048]{1,0:T(8,128)(2,1)S(1)}) custom-call(bf16[2,512,2048]{2,1,0:T(8,128)(2,1)} %bitcast.6, s32[4]{0:T(128)} %refs_1_.1, s32[4]{0:T(128)} %refs_2_.1, s32[4,8]{1,0:T(4,128)} %refs_3_.1, s32[4]{0:T(128)} %refs_4_.1, f32[8,64,64]{2,1,0:T(8,128)} %bitcast.9), custom_call_target="tpu_custom_call" | custom-call | bytes 2228224 | tf_op jit(solution)/shard_map/pallas_call | solution.py:27
  7.0 0.7 %collective-permute-done.1.near_ref = bf16[64,640]{1,0:T(8,128)(2,1)S(1)} collective-permute-done((bf16[64,640]{1,0:T(8,128)(2,1)S(1)}, bf16[64,640]{1,0:T(8,128)(2,1)S(1)}, u32[]{:S(2)}, u32[]{:S(2)}) %collective-permute-start.1) | collective-permute-done | bytes 81952 | tf_op jit(solution)/shard_map/ppermute | solution.py:265
  7.7 2.0 %collective-permute-start.2 = (bf16[64,768]{1,0:T(8,128)(2,1)S(1)}, bf16[64,768]{1,0:T(8,128)(2,1)S(1)}, u32[]{:S(2)}, u32[]{:S(2)}) collective-permute-start(bf16[64,768]{1,0:T(8,128)(2,1)S(1)} %shard_map.93.after_ref), channel_id=1, source_target_pairs={{0,4},{1,9},{2,6},{3,11},{4,0},{5,13},{6,2},{7,15},{8,12},{9,1},{1... | collective-permute-start | bytes 294920 | tf_op jit(solution)/shard_map/ppermute | solution.py:265
  9.7 1.5 %collective-permute-start = (bf16[64,512]{1,0:T(8,128)(2,1)S(1)}, bf16[64,512]{1,0:T(8,128)(2,1)S(1)}, u32[]{:S(2)}, u32[]{:S(2)}) collective-permute-start(bf16[64,512]{1,0:T(8,128)(2,1)S(1)} %get-tuple-element.17), channel_id=1, source_target_pairs={{0,2},{1,3},{2,0},{3,1},{4,6},{5,7},{6,4},{7,5},{8,10},{9,11},{10,... | collective-permute-start | bytes 196616 | tf_op jit(solution)/shard_map/ppermute | solution.py:251
  11.2 0.2 shard_map.94
  11.4 1.0 %collective-permute-done.2.far_ref = bf16[64,768]{1,0:T(8,128)(2,1)S(1)} collective-permute-done((bf16[64,768]{1,0:T(8,128)(2,1)S(1)}, bf16[64,768]{1,0:T(8,128)(2,1)S(1)}, u32[]{:S(2)}, u32[]{:S(2)}) %collective-permute-start.2) | collective-permute-done | bytes 98336 | tf_op jit(solution)/shard_map/ppermute | solution.py:265
  12.4 0.2 shard_map.95
  12.6 1.4 %collective-permute-done = bf16[64,512]{1,0:T(8,128)(2,1)S(1)} collective-permute-done((bf16[64,512]{1,0:T(8,128)(2,1)S(1)}, bf16[64,512]{1,0:T(8,128)(2,1)S(1)}, u32[]{:S(2)}, u32[]{:S(2)}) %collective-permute-start) | collective-permute-done | bytes 65568 | tf_op jit(solution)/shard_map/ppermute | solution.py:251
  14.0 0.1 collective-permute-start.3
  14.1 1.6 %collective-permute-start.4 = (bf16[64,640]{1,0:T(8,128)(2,1)S(1)}, bf16[64,640]{1,0:T(8,128)(2,1)S(1)}, u32[]{:S(2)}, u32[]{:S(2)}) collective-permute-start(bf16[64,640]{1,0:T(8,128)(2,1)S(1)} %shard_map.95), channel_id=1, source_target_pairs={{0,2},{1,3},{2,0},{3,1},{4,6},{5,7},{6,4},{7,5},{8,10},{9,11},{10,... | collective-permute-start | bytes 245768 | tf_op jit(solution)/shard_map/ppermute | solution.py:251
  15.6 3.3 %collective-permute-done.4.late_ref = bf16[64,640]{1,0:T(8,128)(2,1)S(1)} collective-permute-done((bf16[64,640]{1,0:T(8,128)(2,1)S(1)}, bf16[64,640]{1,0:T(8,128)(2,1)S(1)}, u32[]{:S(2)}, u32[]{:S(2)}) %collective-permute-start.4) | collective-permute-done | bytes 81952 | tf_op jit(solution)/shard_map/ppermute | solution.py:251
  18.9 0.0 collective-permute-start.5
  18.9 1.9 %shard_map.96 = (f32[64,512]{1,0:T(8,128)S(1)}, bf16[512,2048]{1,0:T(8,128)(2,1)S(1)}, bf16[64,512]{1,0:T(8,128)(2,1)S(1)}) custom-call(bf16[64,1664]{1,0:T(8,128)(2,1)S(1)} %pad_maximum_fusion.held_ref.mine_ref, bf16[512,2048]{1,0:T(8,128)(2,1)S(1)} %get-tuple-element.22.own_ref, ...), custom_call_target="tpu_custom_call", output_to_operand_aliasing={{1}: (2, {})} | custom-call | flops 134217728 | bytes 2097152 | tf_op jit(solution)/shard_map/pallas_call | solution.py:27
  20.8 0.0 collective-permute-done.3.early_ref
  20.9 1.0 %shard_map.98 = (f32[64,512]{1,0:T(8,128)S(1)}, f32[64,64]{1,0:T(8,128)S(1)}) custom-call(f32[64,512]{1,0:T(8,128)S(1)} %shard_map.97.sum_ref, bf16[64,1664]{1,0:T(8,128)(2,1)S(1)} %pad_maximum_fusion.held_ref.mine_ref, bf16[64,1664]{1,0:T(8,128)(2,1)S(1)} %collective-permute-done.3.early_ref, bf16[64,640]{1,0:T(8,128)(2,1)S(1)} %collective-permute-done.4.late_ref, ...), custom_call_target="tpu_custom_call" | custom-call | flops 134217728 | bytes 2097152 | tf_op jit(solution)/shard_map/pallas_call | solution.py:27
  21.8 0.0 collective-permute-done.5.other_ref
  21.9 1.0 %shard_map.99 = f32[64,512]{1,0:T(8,128)} custom-call(f32[64,512]{1,0:T(8,128)S(1)} %get-tuple-element.26.sum_ref, f32[64,64]{1,0:T(8,128)S(1)} %get-tuple-element.27.core_ref, bf16[64,640]{1,0:T(8,128)(2,1)S(1)} %collective-permute-done.5.other_ref, bf16[64,512]{1,0:T(8,128)(2,1)S(1)} %get-tuple-element.28.basis_ref, ...), custom_call_target="tpu_custom_call" | custom-call | flops 134217728 | bytes 2097152 | tf_op jit(solution)/shard_map/pallas_call | solution.py:27
  (3 shorter events, 0.1 us)
Async XLA Ops:
  1.1 6.6 %collective-permute-start.1 = (bf16[64,640]{1,0:T(8,128)(2,1)S(1)}, bf16[64,640]{1,0:T(8,128)(2,1)S(1)}, u32[]{:S(2)}, u32[]{:S(2)}) collective-permute-start(bf16[64,640]{1,0:T(8,128)(2,1)S(1)} %get-tuple-element.20.mine_ref), channel_id=1, source_target_pairs={{0,8},{1,5},{2,10},{3,7},{4,12},{5,1},{6,14},{7,3},{8,0},{9,13},{1... | collective-permute-start | bytes 245768 | tf_op jit(solution)/shard_map/ppermute | solution.py:265
  7.7 4.7 %collective-permute-start.2 = (bf16[64,768]{1,0:T(8,128)(2,1)S(1)}, bf16[64,768]{1,0:T(8,128)(2,1)S(1)}, u32[]{:S(2)}, u32[]{:S(2)}) collective-permute-start(bf16[64,768]{1,0:T(8,128)(2,1)S(1)} %shard_map.93.after_ref), channel_id=1, source_target_pairs={{0,4},{1,9},{2,6},{3,11},{4,0},{5,13},{6,2},{7,15},{8,12},{9,1},{1... | collective-permute-start | bytes 294920 | tf_op jit(solution)/shard_map/ppermute | solution.py:265
  9.7 4.3 %collective-permute-start = (bf16[64,512]{1,0:T(8,128)(2,1)S(1)}, bf16[64,512]{1,0:T(8,128)(2,1)S(1)}, u32[]{:S(2)}, u32[]{:S(2)}) collective-permute-start(bf16[64,512]{1,0:T(8,128)(2,1)S(1)} %get-tuple-element.17), channel_id=1, source_target_pairs={{0,2},{1,3},{2,0},{3,1},{4,6},{5,7},{6,4},{7,5},{8,10},{9,11},{10,... | collective-permute-start | bytes 196616 | tf_op jit(solution)/shard_map/ppermute | solution.py:251
  14.0 6.8 %collective-permute-start.3 = (bf16[64,1664]{1,0:T(8,128)(2,1)S(1)}, bf16[64,1664]{1,0:T(8,128)(2,1)S(1)}, u32[]{:S(2)}, u32[]{:S(2)}) collective-permute-start(bf16[64,1664]{1,0:T(8,128)(2,1)S(1)} %pad_maximum_fusion.held_ref.mine_ref), channel_id=1, source_target_pairs={{0,1},{1,0},{2,3},{3,2},{4,5},{5,4},{6,7},{7,6},{8,9},{9,8},{10,11... | collective-permute-start | bytes 638984 | tf_op jit(solution)/shard_map/ppermute | solution.py:251
  14.1 4.8 %collective-permute-start.4 = (bf16[64,640]{1,0:T(8,128)(2,1)S(1)}, bf16[64,640]{1,0:T(8,128)(2,1)S(1)}, u32[]{:S(2)}, u32[]{:S(2)}) collective-permute-start(bf16[64,640]{1,0:T(8,128)(2,1)S(1)} %shard_map.95), channel_id=1, source_target_pairs={{0,2},{1,3},{2,0},{3,1},{4,6},{5,7},{6,4},{7,5},{8,10},{9,11},{10,... | collective-permute-start | bytes 245768 | tf_op jit(solution)/shard_map/ppermute | solution.py:251
  18.9 2.9 %collective-permute-start.5 = (bf16[64,640]{1,0:T(8,128)(2,1)S(1)}, bf16[64,640]{1,0:T(8,128)(2,1)S(1)}, u32[]{:S(2)}, u32[]{:S(2)}) collective-permute-start(bf16[64,640]{1,0:T(8,128)(2,1)S(1)} %collective-permute-done.4.late_ref), channel_id=1, source_target_pairs={{0,1},{1,0},{2,3},{3,2},{4,5},{5,4},{6,7},{7,6},{8,9},{9,8},{10,11... | collective-permute-start | bytes 245768 | tf_op jit(solution)/shard_map/ppermute | solution.py:251

commit v7 on v5

--- a/solution.py
+++ b/solution.py
@@ -10,7 +10,7 @@
 
 REACH = 2
 PIECES = 3
-CUTS = 2
+CUTS = 4
 F32 = jnp.float32
 BF16 = jnp.bfloat16
 VMEM = pl.BlockSpec(memory_space=pltpu.VMEM)
@@ -82,12 +82,12 @@
     for copy in copies:
         copy.wait()
     rounded = grad_ref[...].astype(BF16)
-    out_ref[:, :rows] = rounded
-    own_ref[...] = rounded
     basis = basis_ref[...]
     doubled = jnp.concatenate((basis, basis), axis=0)
     partial = lax.dot_general(rounded, doubled, NT, preferred_element_type=F32)
     out_ref[:, rows:] = twins(partial)
+    out_ref[:, :rows] = rounded
+    own_ref[...] = rounded
 
 
 def table_kernel(*refs):
@@ -187,7 +187,7 @@
     sum_ref, mine_ref, early_ref, late_ref, own_ref, tiles_ref, out_ref, core_ref, *, early, late, cores
 ):
     tiles = (own_ref, tiles_ref)
-    out_ref[...] = near(near(sum_ref[...], late_ref, tiles, late), early_ref, tiles, early)
+    out_ref[...] = near(near(sum_ref[...], early_ref, tiles, early), late_ref, tiles, late)
     core = jnp.zeros(core_ref.shape, F32)
     for ref, lanes in zip((mine_ref, early_ref, late_ref), cores):
         for lane in lanes:
@@ -198,9 +198,9 @@
 def last_kernel(
     sum_ref, core_ref, other_ref, basis_ref, own_ref, tiles_ref, out_ref, *, late, lane
 ):
+    total = near(sum_ref[...], other_ref, (own_ref, tiles_ref), late)
     core = (core_ref[...] + join(other_ref, lane, core_ref.shape[1])).astype(BF16)
-    far = jnp.dot(core, basis_ref[...], preferred_element_type=F32)
-    out_ref[...] = near(sum_ref[...] + far, other_ref, (own_ref, tiles_ref), late)
+    out_ref[...] = total + jnp.dot(core, basis_ref[...], preferred_element_type=F32)
 
 
 def swap(value, axis, step):

time: 22.9 us -> 22.8 us (level)
  no operation moved by 1% of the time
where the time goes in v7:
time: 22.8 us; the launch traced here: 22.6 us
  starting transfers between devices  9.23 us (40%)
  Pallas kernels  6.88 us (30%)
  waiting for transfers between devices  6.37 us (28%)
    pallas_call x8, Pallas kernels, call(): pl.pallas_call(kernel, out_shape=out, in_specs=specs, out_specs=jax.tree....  6.88 us
    ppermute x2, starting transfers between devices, crossed(): return lax.ppermute(value, ('cell', 'col'), pairs)  6.1 us
    ppermute x4, waiting for transfers between devices, swap(): return lax.ppermute(value, axis, [(i, i ^ step) for i in range(size)])  4.66 us
    ppermute x4, starting transfers between devices, swap(): return lax.ppermute(value, axis, [(i, i ^ step) for i in range(size)])  3.13 us
    ppermute x2, waiting for transfers between devices, crossed(): return lax.ppermute(value, ('cell', 'col'), pairs)  1.71 us
  transfers between devices with their start and end apart: 6, of which 4 were waited for; matrix products, arithmetic and copies ran while one was open for 0% of the time, Pallas kernels for 21%

profile of v7, /device:TPU:0, one launch (start us, length us, event | category | flops | bytes accessed | tf_op | source)
XLA Modules:
  0.0 22.6 jit_solution(16816354041311845166)
XLA Ops:
  0.0 1.1 %shard_map.91 = (bf16[64,640]{1,0:T(8,128)(2,1)S(1)}, bf16[64,512]{1,0:T(8,128)(2,1)S(1)}) custom-call(f32[64,512]{1,0:T(8,128)} %bitcast.9, bf16[64,512]{1,0:T(8,128)(2,1)} %bitcast.11), custom_call_target="tpu_custom_call" | custom-call | bytes 262144 | tf_op jit(solution)/shard_map/pallas_call | solution.py:26
  1.1 4.1 %collective-permute-start.1 = (bf16[64,640]{1,0:T(8,128)(2,1)S(1)}, bf16[64,640]{1,0:T(8,128)(2,1)S(1)}, u32[]{:S(2)}, u32[]{:S(2)}) collective-permute-start(bf16[64,640]{1,0:T(8,128)(2,1)S(1)} %get-tuple-element.18.mine_ref), channel_id=1, source_target_pairs={{0,8},{1,5},{2,10},{3,7},{4,12},{5,1},{6,14},{7,3},{8,0},{9,13},{1... | collective-permute-start | bytes 245768 | tf_op jit(solution)/shard_map/ppermute | solution.py:222
  5.2 1.7 %shard_map.92 = (bf16[2,768,128]{2,1,0:T(8,128)(2,1)S(1)}, f32[3,8,128]{2,1,0:T(8,128)S(1)}, bf16[512,2048]{1,0:T(8,128)(2,1)S(1)}) custom-call(bf16[2,512,2048]{2,1,0:T(8,128)(2,1)} %bitcast.6, s32[4]{0:T(128)} %refs_1_.1, s32[4]{0:T(128)} %refs_2_.1, s32[4,8]{1,0:T(4,128)} %refs_3_.1, s32[4]{0:T(128)} %refs_4_.1, f32[8,64,64]{2,1,0:T(8,128)} %bitcast.8), custom_call_target="tpu_custom_call" | custom-call | bytes 2228224 | tf_op jit(solution)/shard_map/pallas_call | solution.py:26
  7.0 0.7 %collective-permute-done.1.near_ref = bf16[64,640]{1,0:T(8,128)(2,1)S(1)} collective-permute-done((bf16[64,640]{1,0:T(8,128)(2,1)S(1)}, bf16[64,640]{1,0:T(8,128)(2,1)S(1)}, u32[]{:S(2)}, u32[]{:S(2)}) %collective-permute-start.1) | collective-permute-done | bytes 81952 | tf_op jit(solution)/shard_map/ppermute | solution.py:222
  7.7 2.0 %collective-permute-start.2 = (bf16[64,768]{1,0:T(8,128)(2,1)S(1)}, bf16[64,768]{1,0:T(8,128)(2,1)S(1)}, u32[]{:S(2)}, u32[]{:S(2)}) collective-permute-start(bf16[64,768]{1,0:T(8,128)(2,1)S(1)} %shard_map.93.after_ref), channel_id=1, source_target_pairs={{0,4},{1,9},{2,6},{3,11},{4,0},{5,13},{6,2},{7,15},{8,12},{9,1},{1... | collective-permute-start | bytes 294920 | tf_op jit(solution)/shard_map/ppermute | solution.py:222
  9.7 1.5 %collective-permute-start = (bf16[64,512]{1,0:T(8,128)(2,1)S(1)}, bf16[64,512]{1,0:T(8,128)(2,1)S(1)}, u32[]{:S(2)}, u32[]{:S(2)}) collective-permute-start(bf16[64,512]{1,0:T(8,128)(2,1)S(1)} %get-tuple-element.15), channel_id=1, source_target_pairs={{0,2},{1,3},{2,0},{3,1},{4,6},{5,7},{6,4},{7,5},{8,10},{9,11},{10,... | collective-permute-start | bytes 196616 | tf_op jit(solution)/shard_map/ppermute | solution.py:208
  11.2 0.2 shard_map.94.core_ref
  11.4 1.0 %collective-permute-done.2.far_ref = bf16[64,768]{1,0:T(8,128)(2,1)S(1)} collective-permute-done((bf16[64,768]{1,0:T(8,128)(2,1)S(1)}, bf16[64,768]{1,0:T(8,128)(2,1)S(1)}, u32[]{:S(2)}, u32[]{:S(2)}) %collective-permute-start.2) | collective-permute-done | bytes 98336 | tf_op jit(solution)/shard_map/ppermute | solution.py:222
  12.4 0.2 shard_map.95
  12.6 1.4 %collective-permute-done = bf16[64,512]{1,0:T(8,128)(2,1)S(1)} collective-permute-done((bf16[64,512]{1,0:T(8,128)(2,1)S(1)}, bf16[64,512]{1,0:T(8,128)(2,1)S(1)}, u32[]{:S(2)}, u32[]{:S(2)}) %collective-permute-start) | collective-permute-done | bytes 65568 | tf_op jit(solution)/shard_map/ppermute | solution.py:208
  14.0 0.1 collective-permute-start.3
  14.1 1.6 %collective-permute-start.4 = (bf16[64,640]{1,0:T(8,128)(2,1)S(1)}, bf16[64,640]{1,0:T(8,128)(2,1)S(1)}, u32[]{:S(2)}, u32[]{:S(2)}) collective-permute-start(bf16[64,640]{1,0:T(8,128)(2,1)S(1)} %shard_map.95), channel_id=1, source_target_pairs={{0,2},{1,3},{2,0},{3,1},{4,6},{5,7},{6,4},{7,5},{8,10},{9,11},{10,... | collective-permute-start | bytes 245768 | tf_op jit(solution)/shard_map/ppermute | solution.py:208
  15.6 3.3 %collective-permute-done.4.late_ref = bf16[64,640]{1,0:T(8,128)(2,1)S(1)} collective-permute-done((bf16[64,640]{1,0:T(8,128)(2,1)S(1)}, bf16[64,640]{1,0:T(8,128)(2,1)S(1)}, u32[]{:S(2)}, u32[]{:S(2)}) %collective-permute-start.4) | collective-permute-done | bytes 81952 | tf_op jit(solution)/shard_map/ppermute | solution.py:208
  18.9 0.0 collective-permute-start.5
  18.9 1.9 %shard_map.96 = (f32[64,512]{1,0:T(8,128)S(1)}, bf16[512,2048]{1,0:T(8,128)(2,1)S(1)}, bf16[64,512]{1,0:T(8,128)(2,1)S(1)}) custom-call(bf16[64,1664]{1,0:T(8,128)(2,1)S(1)} %pad_maximum_fusion.held_ref.mine_ref, bf16[512,2048]{1,0:T(8,128)(2,1)S(1)} %get-tuple-element.19.own_ref, bf16[2,512,2048]{2,1,0:T(8,128)(2,1)} %bitcast.7, bf16[64,512]{1,0:T(8,128)(2,1)} %bitcast.10), custom_call_target="tpu_custom_call" | custom-call | flops 134217728 | bytes 2097152 | tf_op jit(solution)/shard_map/pallas_call | solution.py:26
  20.8 0.0 collective-permute-done.3.early_ref
  20.8 0.8 %shard_map.97 = (f32[64,512]{1,0:T(8,128)S(1)}, f32[64,64]{1,0:T(8,128)S(1)}) custom-call(f32[64,512]{1,0:T(8,128)S(1)} %get-tuple-element.20.sum_ref, bf16[64,1664]{1,0:T(8,128)(2,1)S(1)} %pad_maximum_fusion.held_ref.mine_ref, bf16[64,1664]{1,0:T(8,128)(2,1)S(1)} %collective-permute-done.3.early_ref, bf16[64,640]{1,0:T(8,128)(2,1)S(1)} %collective-permute-done.4.late_ref, ...), custom_call_target="tpu_custom_call" | custom-call | flops 134217728 | bytes 2097152 | tf_op jit(solution)/shard_map/pallas_call | solution.py:26
  21.6 0.0 collective-permute-done.5.other_ref
  21.6 1.0 %shard_map.98 = f32[64,512]{1,0:T(8,128)} custom-call(f32[64,512]{1,0:T(8,128)S(1)} %get-tuple-element.22.sum_ref, f32[64,64]{1,0:T(8,128)S(1)} %get-tuple-element.23.core_ref, bf16[64,640]{1,0:T(8,128)(2,1)S(1)} %collective-permute-done.5.other_ref, bf16[64,512]{1,0:T(8,128)(2,1)S(1)} %get-tuple-element.24.basis_ref, ...), custom_call_target="tpu_custom_call" | custom-call | flops 134217728 | bytes 2097152 | tf_op jit(solution)/shard_map/pallas_call | solution.py:26
  (2 shorter events, 0.1 us)
Async XLA Ops:
  1.1 6.6 %collective-permute-start.1 = (bf16[64,640]{1,0:T(8,128)(2,1)S(1)}, bf16[64,640]{1,0:T(8,128)(2,1)S(1)}, u32[]{:S(2)}, u32[]{:S(2)}) collective-permute-start(bf16[64,640]{1,0:T(8,128)(2,1)S(1)} %get-tuple-element.18.mine_ref), channel_id=1, source_target_pairs={{0,8},{1,5},{2,10},{3,7},{4,12},{5,1},{6,14},{7,3},{8,0},{9,13},{1... | collective-permute-start | bytes 245768 | tf_op jit(solution)/shard_map/ppermute | solution.py:222
  7.7 4.7 %collective-permute-start.2 = (bf16[64,768]{1,0:T(8,128)(2,1)S(1)}, bf16[64,768]{1,0:T(8,128)(2,1)S(1)}, u32[]{:S(2)}, u32[]{:S(2)}) collective-permute-start(bf16[64,768]{1,0:T(8,128)(2,1)S(1)} %shard_map.93.after_ref), channel_id=1, source_target_pairs={{0,4},{1,9},{2,6},{3,11},{4,0},{5,13},{6,2},{7,15},{8,12},{9,1},{1... | collective-permute-start | bytes 294920 | tf_op jit(solution)/shard_map/ppermute | solution.py:222
  9.7 4.3 %collective-permute-start = (bf16[64,512]{1,0:T(8,128)(2,1)S(1)}, bf16[64,512]{1,0:T(8,128)(2,1)S(1)}, u32[]{:S(2)}, u32[]{:S(2)}) collective-permute-start(bf16[64,512]{1,0:T(8,128)(2,1)S(1)} %get-tuple-element.15), channel_id=1, source_target_pairs={{0,2},{1,3},{2,0},{3,1},{4,6},{5,7},{6,4},{7,5},{8,10},{9,11},{10,... | collective-permute-start | bytes 196616 | tf_op jit(solution)/shard_map/ppermute | solution.py:208
  14.0 6.8 %collective-permute-start.3 = (bf16[64,1664]{1,0:T(8,128)(2,1)S(1)}, bf16[64,1664]{1,0:T(8,128)(2,1)S(1)}, u32[]{:S(2)}, u32[]{:S(2)}) collective-permute-start(bf16[64,1664]{1,0:T(8,128)(2,1)S(1)} %pad_maximum_fusion.held_ref.mine_ref), channel_id=1, source_target_pairs={{0,1},{1,0},{2,3},{3,2},{4,5},{5,4},{6,7},{7,6},{8,9},{9,8},{10,11... | collective-permute-start | bytes 638984 | tf_op jit(solution)/shard_map/ppermute | solution.py:208
  14.1 4.8 %collective-permute-start.4 = (bf16[64,640]{1,0:T(8,128)(2,1)S(1)}, bf16[64,640]{1,0:T(8,128)(2,1)S(1)}, u32[]{:S(2)}, u32[]{:S(2)}) collective-permute-start(bf16[64,640]{1,0:T(8,128)(2,1)S(1)} %shard_map.95), channel_id=1, source_target_pairs={{0,2},{1,3},{2,0},{3,1},{4,6},{5,7},{6,4},{7,5},{8,10},{9,11},{10,... | collective-permute-start | bytes 245768 | tf_op jit(solution)/shard_map/ppermute | solution.py:208
  18.9 2.7 %collective-permute-start.5 = (bf16[64,640]{1,0:T(8,128)(2,1)S(1)}, bf16[64,640]{1,0:T(8,128)(2,1)S(1)}, u32[]{:S(2)}, u32[]{:S(2)}) collective-permute-start(bf16[64,640]{1,0:T(8,128)(2,1)S(1)} %collective-permute-done.4.late_ref), channel_id=1, source_target_pairs={{0,1},{1,0},{2,3},{3,2},{4,5},{5,4},{6,7},{7,6},{8,9},{9,8},{10,11... | collective-permute-start | bytes 245768 | tf_op jit(solution)/shard_map/ppermute | solution.py:208
